TPU v7x, 128 devices: a whole 4x4x4 slice. The times are simulated.
128 devices in a mesh: skyx: 4 (over z_lo, core), skyy: 8 (over z_hi, y), be: 4 (over x).
Axes of the slice: x: 4, y: 4, z: 4 (z_hi: 2, z_lo: 2; z = z_hi * 2 + z_lo), core: 2. Of those that a mesh axis runs over, the one named last changes fastest.
Arguments:
- image: float32 [4, 1024, 2048], P('be', 'skyx', 'skyy'), may hold values from -6 to 6
- psf_taps: float32 [4, 2, 15], P('be'), may hold values from 0.1 to 1
- exposure_weight: float32 [4], P('be'), may hold values from 0.5 to 4
- flux_start: float32 [4, 8, 16], P('skyx', 'skyy'), may hold values from 1 to 4
- centre_shift: float32 [2, 4, 8, 16], P(None, 'skyx', 'skyy'), may hold values from -0.5 to 0.5
- radius: float32 [4, 8, 16], P('skyx', 'skyy'), may hold values from 1.5 to 6
- ellipticity: float32 [2, 4, 8, 16], P(None, 'skyx', 'skyy'), may hold values from -0.4 to 0.4
- offsets: int32 [2, 4, 8, 16], P(None, 'skyx', 'skyy'), may hold values from -32 to 223, as said below
- source_count: int32 [4, 8], P('skyx', 'skyy'), may hold values from 4 to 16, as said below
Outputs:
- refined: float32 [3, 4, 8, 16], P(None, 'skyx', 'skyy')
- residual: float32 [4, 1024, 2048], P('be', 'skyx', 'skyy')
Inputs may be any that keep to these rules, and one draw needn't show every extreme that they name: `offsets`: stamp corners in the tile's own pixels; a stamp's middle pixel lies in its tile; among the live sources of a tile at most 4 have stamps that reach past the tile's edge, and some tile has exactly 4. Slots 0 to source_count - 1 of a tile hold its sources and the rest are empty; some tile is full.
All inputs are finite; a program needn't handle non-finite values.
Results may differ from a plain program's by a relative error of at most 0.0003.
Values sent between devices are 32-bit elements; how exact they have to be, the bound alone decides.
A program may use at most 64 MiB of HBM per device.

v0:
```python
import jax
import jax.numpy as jnp
from jax import lax
from jax.sharding import PartitionSpec as P

STAMP = 64


HIGHEST = lax.Precision.HIGHEST
PRIOR = 8.0


def padded_2(block, sides, width):
    for axis, dim in sides:
        count = lax.axis_size(axis)
        forward = [(i, i + 1) for i in range(count - 1)]
        backward = [(target, source) for source, target in forward]
        low = lax.ppermute(
            lax.slice_in_dim(block, block.shape[dim] - width, None, axis=dim), axis, forward
        )
        high = lax.ppermute(lax.slice_in_dim(block, 0, width, axis=dim), axis, backward)
        block = jnp.concatenate([low, block, high], axis=dim)
    return block


def psf_matrix(taps, size):
    width = taps.shape[0]
    reach = (width - 1) // 2
    grid = jnp.arange(size, dtype=jnp.int32)
    differ = grid[:, None] - grid[None, :] + reach
    picks = (differ[:, :, None] == jnp.arange(width, dtype=jnp.int32)[None, None, :]).astype(
        jnp.float32
    )
    return jnp.sum(picks * taps[None, None, :], axis=-1) / jnp.sum(taps)


def profiles(shift_x, shift_y, radius, ellipse_one, ellipse_two, size):
    grid = jnp.arange(size, dtype=jnp.float32)
    middle = float(size // 2)
    along_x = grid[:, None] - (middle + shift_x)[None, :]
    along_y = grid[None, :] - (middle + shift_y)[:, None]
    inverse = 1.0 / (radius * radius)
    coef_a = ((1.0 + ellipse_one) * inverse)[None, :, None]
    coef_b = (ellipse_two * inverse)[None, :, None]
    coef_c = ((1.0 - ellipse_one) * inverse)[None, :, None]
    upper = along_x[:, :, None]
    lower = along_y[None, :, :]
    root = jnp.sqrt(
        coef_a * upper * upper + 2.0 * coef_b * upper * lower + coef_c * lower * lower + 0.25
    )
    profile = jnp.exp(-root)
    return (
        profile,
        profile * (coef_a * upper + coef_b * lower) / root,
        profile * (coef_b * upper + coef_c * lower) / root,
    )


def blur(stack, first, second):
    size = stack.shape[0]
    along_rows = jnp.dot(
        first, stack.reshape(size, -1), precision=HIGHEST, preferred_element_type=jnp.float32
    )
    along_columns = jnp.dot(
        along_rows.reshape(-1, size),
        second.T,
        precision=HIGHEST,
        preferred_element_type=jnp.float32,
    )
    return along_columns.reshape(stack.shape)


def place(canvas, stamps, row_index, column_index):
    height = canvas.shape[0]
    width = canvas.shape[1]
    row_index = jnp.where((row_index >= 0) & (row_index < height), row_index, height)
    column_index = jnp.where((column_index >= 0) & (column_index < width), column_index, width)
    return canvas.at[row_index[:, :, None], column_index[None, :, :]].add(stamps, mode="drop")


def solve_three(matrix, right):

    def adjugate(row, column):
        return (
            matrix[(column + 1) % 3, (row + 1) % 3] * matrix[(column + 2) % 3, (row + 2) % 3]
            - matrix[(column + 1) % 3, (row + 2) % 3] * matrix[(column + 2) % 3, (row + 1) % 3]
        )

    determinant = (
        matrix[0, 0] * adjugate(0, 0)
        + matrix[0, 1] * adjugate(1, 0)
        + matrix[0, 2] * adjugate(2, 0)
    )
    return jnp.stack(
        [
            (
                adjugate(row, 0) * right[0]
                + adjugate(row, 1) * right[1]
                + adjugate(row, 2) * right[2]
            )
            / determinant
            for row in range(3)
        ]
    )


def shards(
    image,
    psf_taps,
    exposure_weight,
    flux_start,
    centre_shift,
    radius,
    ellipticity,
    offsets,
    source_count,
):
    tile = image.shape[1]
    slots = flux_start.shape[2]
    stamp = STAMP
    margin = stamp // 2
    grid = jnp.arange(stamp, dtype=jnp.int32)
    live = (jnp.arange(slots, dtype=jnp.int32) < source_count[0, 0]).astype(jnp.float32)
    flux = flux_start[0, 0] * live
    shift_x = centre_shift[0, 0, 0]
    shift_y = centre_shift[1, 0, 0]
    local_x = offsets[0, 0, 0]
    local_y = offsets[1, 0, 0]
    inside_x = (
        (grid[:, None] + local_x[None, :] >= 0) & (grid[:, None] + local_x[None, :] < tile)
    ).astype(jnp.float32)
    inside_y = (
        (local_y[:, None] + grid[None, :] >= 0) & (local_y[:, None] + grid[None, :] < tile)
    ).astype(jnp.float32)
    mask = inside_x[:, :, None] * inside_y[None, :, :]
    profile, slope_x, slope_y = profiles(
        shift_x, shift_y, radius[0, 0], ellipticity[0, 0, 0], ellipticity[1, 0, 0], stamp
    )
    weighted_flux = flux[None, :, None]
    frames, taps_all, weights = (image, psf_taps, exposure_weight)
    own_rows = grid[:, None] + local_x[None, :] + margin
    own_columns = local_y[:, None] + grid[None, :] + margin
    low_edge = (jnp.arange(tile, dtype=jnp.int32) < margin).astype(jnp.float32)
    high_edge = (jnp.arange(tile, dtype=jnp.int32) >= tile - margin).astype(jnp.float32)
    cut_rows = grid[:, None] + local_x[None, :] + margin
    cut_columns = local_y[:, None] + grid[None, :] + margin
    first = psf_matrix(taps_all[0, 0], stamp)
    second = psf_matrix(taps_all[0, 1], stamp)
    blurred = blur(profile, first, second)
    canvas = place(
        jnp.zeros((tile + stamp, tile + stamp), jnp.float32),
        blurred * weighted_flux,
        own_rows,
        own_columns,
    )
    wider = padded_2(canvas, (("skyx", 0), ("skyy", 1)), margin)
    folded = (
        low_edge[:, None] * wider[0:tile]
        + wider[stamp : stamp + tile]
        + high_edge[:, None] * wider[2 * stamp : 2 * stamp + tile]
    )
    model = (
        folded[:, 0:tile] * low_edge[None, :]
        + folded[:, stamp : stamp + tile]
        + folded[:, 2 * stamp : 2 * stamp + tile] * high_edge[None, :]
    )
    remain = frames[0] - model
    residuals = [remain]
    jacobian = jnp.stack(
        [
            blurred * mask,
            blur(slope_x, first, second) * weighted_flux * mask,
            blur(slope_y, first, second) * weighted_flux * mask,
        ]
    )
    padded = jnp.pad(remain, margin)
    cutout = padded[cut_rows[:, :, None], cut_columns[None, :, :]]
    normal = weights[0] * jnp.einsum("kisj,lisj->kls", jacobian, jacobian, precision=HIGHEST)
    right = weights[0] * jnp.einsum("kisj,isj->ks", jacobian, cutout, precision=HIGHEST)
    normal, right = lax.psum((normal, right), "be")
    identity = jnp.eye(3, dtype=jnp.float32)[:, :, None]
    change = solve_three(normal + PRIOR * identity, right)
    refined = (
        jnp.stack([flux_start[0, 0] + change[0], shift_x + change[1], shift_y + change[2]])
        * live[None, :]
    )
    stacked = jnp.stack(residuals)
    return (refined.reshape(3, 1, 1, slots), stacked)


def solution(mesh):
    return jax.shard_map(
        shards,
        mesh=mesh,
        in_specs=(
            P("be", "skyx", "skyy"),
            P("be", None, None),
            P("be"),
            P("skyx", "skyy", None),
            P(None, "skyx", "skyy", None),
            P("skyx", "skyy", None),
            P(None, "skyx", "skyy", None),
            P(None, "skyx", "skyy", None),
            P("skyx", "skyy"),
        ),
        out_specs=(P(None, "skyx", "skyy", None), P("be", "skyx", "skyy")),
        check_vma=False,
    )
```

profile of v0, /device:TPU:24, one launch (start us, length us, event | category | flops | bytes accessed | tf_op | source)
XLA Modules:
  0.0 1046.3 jit_solution(16624219362513049191)
XLA Ops:
  0.7 0.7 slice_bitcast_fusion.1
  1.6 0.7 bitcast_multiply_fusion.25
  2.3 0.7 broadcast_multiply_fusion.1
  3.3 0.7 add_bitcast_fusion.1
  4.2 1.4 slice_reduce_fusion.9
  6.5 0.5 fusion.22
  7.5 0.2 copy-done.8
  8.0 0.6 fusion.33
  8.6 2.3 fusion.48
  10.8 1.2 broadcast_multiply_fusion
  12.1 0.3 copy.28
  12.5 448.4 %scatter_custom_fusion = f32[102400]{0:T(1024)S(1)} fusion(s32[65536]{0:T(1024)S(1)} %reshape.1001, f32[65536]{0:T(1024)S(1)} %reshape.1003, f32[]{:T(128)} %constant.14.clone.1), kind=kCustom, calls=%fused_computation.55 | custom fusion | flops 65536 | bytes 409604
  461.0 1.7 collective-permute-start
  462.9 1.5 collective-permute-start.1
  464.3 2.3 fusion.44
  466.6 1.2 fusion.5
  467.8 2.3 fusion.46
  470.1 1.2 fusion.7
  472.3 10.1 fusion.14
  482.6 0.6 fusion.75
  483.6 2.6 collective-permute-start.3
  486.2 7.0 collective-permute-start.2
  493.3 0.5 compare_convert_fusion.2
  493.9 0.8 collective-permute-done.3
  494.7 1.7 collective-permute-done.2
  496.4 0.3 pad_maximum_fusion.1
  497.0 0.7 copy-done.2
  497.9 519.5 %gather_fusion = f32[65536]{0:T(1024)S(1)} fusion(f32[320,320]{1,0:T(8,128)S(1)} %pad.4, s32[65536]{0:T(1024)S(1)} %reshape.995), kind=kCustom, calls=%fused_computation | custom fusion | bytes 1048576 | tf_op jit(solution)/shard_map/gather | solution.py:177
  1017.7 10.1 fusion
  1027.9 17.3 %all-reduce.1 = (f32[3,3,16]{0,1,2:T(4,128)S(1)}, f32[3,16]{1,0:T(4,128)S(1)}) all-reduce(f32[3,3,16]{0,1,2:T(4,128)S(1)} %copy-done.4, f32[3,16]{1,0:T(4,128)S(1)} %fusion.74), channel_id=1, replica_groups=mesh['skyx'=4,'skyy'=8,'be'=4] {'be'}, use_global_device_ids=true, to_apply=%region_4.5 | all-reduce | flops 192 | bytes 1536 | tf_op jit(solution)/shard_map/psum | solution.py:180
  1045.2 0.4 slice_reduce_fusion.4
  1045.8 0.6 maximum_multiply_fusion
  (69 shorter events, 3.8 us)
Async XLA Ops:
  0.6 6.4 copy-start.7
  7.0 0.7 copy-start.8
  461.0 22.3 %collective-permute-start = (f32[32,320]{1,0:T(8,128)S(1)}, f32[32,320]{1,0:T(8,128)S(1)}, u32[]{:S(2)}, u32[]{:S(2)}) collective-permute-start(f32[32,320]{1,0:T(8,128)S(1)} %reshape.993), channel_id=1, source_target_pairs={{0,32},{32,64},{64,96},{1,33},{33,65},{65,97},{2,34},{34,66},{66,9... | collective-permute-start | bytes 122888 | tf_op jit(solution)/shard_map/ppermute | solution.py:18
  462.9 20.6 %collective-permute-start.1 = (f32[32,320]{1,0:T(8,128)S(1)}, f32[32,320]{1,0:T(8,128)S(1)}, u32[]{:S(2)}, u32[]{:S(2)}) collective-permute-start(f32[32,320]{1,0:T(8,128)S(1)} %reshape.994), channel_id=1, source_target_pairs={{32,0},{64,32},{96,64},{33,1},{65,33},{97,65},{34,2},{66,34},{98,6... | collective-permute-start | bytes 122888 | tf_op jit(solution)/shard_map/ppermute | solution.py:21
  472.2 10.4 copy-start
  483.6 11.2 %collective-permute-start.3 = (f32[384,32]{1,0:T(8,128)S(1)}, f32[384,32]{1,0:T(8,128)S(1)}, u32[]{:S(2)}, u32[]{:S(2)}) collective-permute-start(f32[384,32]{1,0:T(8,128)S(1)} %get-tuple-element.30), channel_id=1, source_target_pairs={{4,0},{8,4},{12,8},{16,12},{20,16},{24,20},{28,24},{5,1},{9,5},{13... | collective-permute-start | bytes 147464 | tf_op jit(solution)/shard_map/ppermute | solution.py:21
  486.2 10.2 collective-permute-start.2
  493.9 3.0 copy-start.3
  497.0 0.7 copy-start.2
  497.9 519.7 %copy-start.1 = (f32[3,64,16,64]{3,1,2,0:T(8,128)S(1)}, f32[3,64,16,64]{3,1,2,0:T(8,128)}, u32[]{:S(2)}) copy-start(f32[3,64,16,64]{3,1,2,0:T(8,128)} %copy-done) | copy-start | bytes 2359300
  1017.6 10.3 copy-start.4
  1017.6 27.6 %copy-start.5 = (f32[3,3]{0,1:T(4,128)S(1)}, f32[3,3]{0,1:T(4,128)}, u32[]{:S(2)}) copy-start(f32[3,3]{0,1:T(4,128)} %fusion.75) | copy-start | bytes 112
  1017.6 28.0 %copy-start.9 = (f32[1,1,16]{2,1,0:T(1,128)S(1)}, f32[1,1,16]{2,1,0:T(1,128)}, u32[]{:S(2)}) copy-start(f32[1,1,16]{2,1,0:T(1,128)} %param.12) | copy-start | bytes 196
  1017.7 28.0 %copy-start.6 = (f32[2,1,1,16]{3,2,1,0:T(1,128)S(1)}, f32[2,1,1,16]{3,2,1,0:T(1,128)}, u32[]{:S(2)}) copy-start(f32[2,1,1,16]{3,2,1,0:T(1,128)} %param.13) | copy-start | bytes 388
  1017.7 28.1 %copy-start.10 = (f32[16]{0:T(128)S(1)}, f32[16]{0:T(128)}, u32[]{:S(2)}) copy-start(f32[16]{0:T(128)} %compare_convert_fusion.2) | copy-start | bytes 196
where the time goes:
time: 1050 us
  local copies, waits for them, and re-layouts  524 us (50%)
  other arithmetic  456 us (43%)
  matrix products  30.7 us (3%)
  blocking collectives  17.3 us (2%)
  starting transfers between devices  12.9 us (1%)
    gather x2, local copies, waits for them, and re-layouts, shards(): cutout = padded[cut_rows[:, :, None], cut_columns[None, :, :]]  520 us
    unnamed x4, other arithmetic  449 us
  transfers between devices with their start and end apart: 4, of which 2 were waited for; matrix products, arithmetic and copies ran while one was open for 2% of the time, Pallas kernels for 0%

commit v1 on v0

v1 whole, which is shorter than its diff:
```python
import jax
import jax.numpy as jnp
from jax import lax
from jax.experimental import pallas as pl
from jax.experimental.pallas import tpu as pltpu
from jax.sharding import PartitionSpec as P

STAMP = 64
MARGIN = 32
TAPS = 15
PRIOR = 8.0
F32 = jnp.float32
BF16 = jnp.bfloat16
MESH = pl.DeviceIdType.MESH


def split(x):
    high = x.astype(BF16)
    return high, (x - high.astype(F32)).astype(BF16)


def band(taps_ref, which, differ):
    total = taps_ref[0, which, 0]
    for t in range(1, TAPS):
        total = total + taps_ref[0, which, t]
    out = jnp.zeros(differ.shape, F32)
    for t in range(TAPS):
        out = jnp.where(differ == t - TAPS // 2, taps_ref[0, which, t], out)
    return out / jnp.full(differ.shape, total, F32)


def kernel(
    image_hbm,
    taps_ref,
    weight_ref,
    flux_ref,
    shift_ref,
    radius_ref,
    ellipse_ref,
    offset_ref,
    count_ref,
    flux_vec,
    shift_vec,
    refined_ref,
    residual_hbm,
    image,
    stacked,
    field,
    blurred,
    lanes_high,
    lanes_low,
    canvas,
    pack_left,
    pack_right,
    in_rows,
    in_sides,
    in_corners,
    remain,
    partial,
    sums,
    copy_sems,
    send_sems,
    recv_sems,
    sum_send,
    sum_recv,
):
    slots = flux_ref.shape[2]
    tile = image_hbm.shape[1]
    pairs = slots // 2
    mx = lax.axis_index("skyx")
    my = lax.axis_index("skyy")
    me = lax.axis_index("be")
    nx = lax.axis_size("skyx")
    ny = lax.axis_size("skyy")
    nb = lax.axis_size("be")
    up, down = lax.rem(mx + nx - 1, nx), lax.rem(mx + 1, nx)
    left, right = lax.rem(my + ny - 1, ny), lax.rem(my + 1, ny)
    around = [
        (up, my, me),
        (down, my, me),
        (mx, left, me),
        (mx, right, me),
        (up, left, me),
        (up, right, me),
        (down, left, me),
        (down, right, me),
    ]
    peers = [(mx, my, lax.rem(me + d, nb)) for d in range(1, nb)]

    barrier = pltpu.get_barrier_semaphore()
    for device in around + peers:
        pl.semaphore_signal(barrier, inc=1, device_id=device, device_id_type=MESH)
    fetch = pltpu.make_async_copy(image_hbm.at[0], image, copy_sems.at[0])
    fetch.start()

    row = lax.broadcasted_iota(jnp.int32, (STAMP, 128), 0)
    lane = lax.broadcasted_iota(jnp.int32, (STAMP, 128), 1)
    lane1 = lax.broadcasted_iota(jnp.int32, (1, 128), 1)
    first_half = lane1 < STAMP
    column1 = jnp.where(first_half, lane1, lane1 - STAMP)
    live_count = count_ref[0, 0]

    def pair_of(ref, *index):
        def at(j):
            return jnp.where(first_half, ref[index + (2 * j,)], ref[index + (2 * j + 1,)])

        return at

    rows_band = band(taps_ref, 0, row[:, :STAMP] - lane[:, :STAMP])
    rows_high, rows_low = split(rows_band)
    left_factor = jnp.concatenate([rows_high, rows_high, rows_low], axis=1)
    columns_band = jnp.where(lane < STAMP, band(taps_ref, 1, lane - row), 0.0)
    columns_next = pltpu.roll(columns_band, STAMP, 1)
    nothing = jnp.zeros((STAMP, 128), F32)
    right_factor = jnp.concatenate(
        [
            jnp.concatenate([columns_band, nothing], axis=1),
            jnp.concatenate([columns_next, nothing], axis=1),
            jnp.concatenate([nothing, columns_band], axis=1),
            jnp.concatenate([nothing, columns_next], axis=1),
        ],
        axis=0,
    )
    right_high, right_low = split(right_factor)

    def blur(count):
        width = count * slots * STAMP
        along = jnp.dot(left_factor, stacked[:, :width], preferred_element_type=F32)
        groups = jnp.concatenate(
            [along[:, 256 * g : 256 * (g + 1)] for g in range(width // 256)], axis=0
        )
        high, low = split(groups)
        out = jnp.dot(high, right_high, preferred_element_type=F32)
        out = out + jnp.dot(low, right_high, preferred_element_type=F32)
        return out + jnp.dot(high, right_low, preferred_element_type=F32)

    def stack(value, start):
        high, low = split(value)
        stacked[0:STAMP, start : start + 128] = high
        stacked[STAMP : 2 * STAMP, start : start + 128] = low
        stacked[2 * STAMP : 3 * STAMP, start : start + 128] = high

    grid_u = row.astype(F32)
    for j in range(pairs):
        shift_x = pair_of(shift_ref, 0, 0, 0)(j)
        shift_y = pair_of(shift_ref, 1, 0, 0)(j)
        radius = pair_of(radius_ref, 0, 0)(j)
        one = pair_of(ellipse_ref, 0, 0, 0)(j)
        two = pair_of(ellipse_ref, 1, 0, 0)(j)
        inverse = 1.0 / (radius * radius)
        coef_a = (1.0 + one) * inverse
        coef_b = two * inverse
        coef_c = (1.0 - one) * inverse
        u = grid_u - (float(STAMP // 2) + shift_x)
        v = column1.astype(F32) - (float(STAMP // 2) + shift_y)
        along_x = coef_a * u + coef_b * v
        along_y = coef_b * u + coef_c * v
        square = u * along_x + v * along_y + 0.25
        inverse_root = lax.rsqrt(square)
        profile = jnp.exp(-(square * inverse_root))
        stack(profile, 128 * j)
        scaled = profile * inverse_root
        field[0, :, 128 * j : 128 * (j + 1)] = scaled * along_x
        field[1, :, 128 * j : 128 * (j + 1)] = scaled * along_y

    spread = blur(1)
    for g in range(slots * STAMP // 256):
        blurred[0, :, 256 * g : 256 * (g + 1)] = spread[STAMP * g : STAMP * (g + 1)]

    targets = []
    for s in range(slots):
        flux = jnp.where(s < live_count, flux_ref[0, 0, s], 0.0)
        at_y = offset_ref[1, 0, 0, s]
        turn = jnp.bitwise_and(at_y, 127)
        block = jnp.right_shift(at_y - turn, 7)
        j, odd = s // 2, s % 2
        value = blurred[0, :, 128 * j : 128 * (j + 1)]
        value = jnp.where(first_half if odd == 0 else ~first_half, value * flux, 0.0)
        value = pltpu.roll(value, jnp.bitwise_and(turn + 128 - STAMP * odd, 127), 1)
        owner = jnp.where(lane1 >= turn, block, block + 1)
        owner = jnp.where(owner == -1, 2, owner)
        for g in range(3):
            high, low = split(jnp.where(owner == g, value, 0.0))
            lanes_high[STAMP * s : STAMP * (s + 1), 128 * g : 128 * (g + 1)] = high
            lanes_low[STAMP * s : STAMP * (s + 1), 128 * g : 128 * (g + 1)] = low
    for j in range(pairs):
        targets.append(pair_of(offset_ref, 0, 0, 0)(j) + column1 + MARGIN)
    target = jnp.concatenate(targets, axis=1)
    rows = tile + 2 * MARGIN
    place = jnp.where(
        lax.broadcasted_iota(jnp.int32, (rows, slots * STAMP), 0) == target, 1.0, 0.0
    ).astype(BF16)
    placed = jnp.dot(place, lanes_high[...], preferred_element_type=F32)
    placed = placed + jnp.dot(place, lanes_low[...], preferred_element_type=F32)
    canvas[...] = placed
    side = placed[MARGIN : MARGIN + tile, 256:384]
    to_left, to_right = None, None
    for c in range(4):
        chunk = side[64 * c : 64 * (c + 1)]
        here = (lane >= 32 * c) & (lane < 32 * (c + 1))
        moved = pltpu.roll(chunk, (32 * c + 128 - 96) % 128, 1)
        to_left = moved if c == 0 else jnp.where(here, moved, to_left)
        moved = pltpu.roll(chunk, 32 * c, 1) if c else chunk
        to_right = moved if c == 0 else jnp.where(here, moved, to_right)
    pack_left[...] = to_left
    pack_right[...] = to_right

    top = canvas.at[0:MARGIN]
    bottom = canvas.at[tile + MARGIN : tile + 2 * MARGIN]
    sources = [
        top.at[:, 0:tile],
        bottom.at[:, 0:tile],
        pack_left,
        pack_right,
        top.at[:, tile : tile + 128],
        top.at[:, tile : tile + 128],
        bottom.at[:, tile : tile + 128],
        bottom.at[:, tile : tile + 128],
    ]
    landings = [
        in_rows.at[0],
        in_rows.at[1],
        in_sides.at[0],
        in_sides.at[1],
        in_corners.at[0],
        in_corners.at[1],
        in_corners.at[2],
        in_corners.at[3],
    ]
    pl.semaphore_wait(barrier, len(around) + len(peers))
    halos = [
        pltpu.make_async_remote_copy(
            src_ref=sources[d],
            dst_ref=landings[d],
            send_sem=send_sems.at[d],
            recv_sem=recv_sems.at[d],
            device_id=around[d],
            device_id_type=MESH,
        )
        for d in range(8)
    ]
    for halo in halos:
        halo.start()

    for k in range(2):
        for j in range(pairs):
            stack(field[k, :, 128 * j : 128 * (j + 1)], 1024 * k + 128 * j)
    spread = blur(2)
    for k in range(2):
        for g in range(4):
            start = STAMP * (4 * k + g)
            blurred[1 + k, :, 256 * g : 256 * (g + 1)] = spread[start : start + STAMP]

    def fold(value):
        total = value[0:8]
        for r in range(8, STAMP, 8):
            total = total + value[r : r + 8]
        return total

    for j in range(pairs):
        at_x = row + pair_of(offset_ref, 0, 0, 0)(j)
        at_y = column1 + pair_of(offset_ref, 1, 0, 0)(j)
        inside = (at_x >= 0) & (at_x < tile) & (at_y >= 0) & (at_y < tile)
        own = slice(128 * j, 128 * (j + 1))
        masked = [jnp.where(inside, blurred[k, :, own], 0.0) for k in range(3)]
        for k in range(3):
            blurred[k, :, own] = masked[k]
        n = 0
        for k in range(3):
            for l in range(k, 3):
                partial[8 * n : 8 * (n + 1), own] = fold(masked[k] * masked[l])
                n += 1

    segment = jnp.where(
        jnp.right_shift(lax.broadcasted_iota(jnp.int32, (slots * STAMP, 128), 0), 6)
        == lax.broadcasted_iota(jnp.int32, (slots * STAMP, 128), 1),
        1.0,
        0.0,
    ).astype(BF16)

    def gather_sums(value):
        high, low = split(value)
        out = jnp.dot(high, segment, preferred_element_type=F32)
        out = out + jnp.dot(low, segment, preferred_element_type=F32)
        return jnp.concatenate(
            [
                jnp.sum(out[8 * k : 8 * (k + 1)], axis=0, keepdims=True)
                for k in range(value.shape[0] // 8)
            ],
            axis=0,
        )

    normal = gather_sums(partial[0:48, :])

    apart = lax.broadcasted_iota(jnp.int32, (STAMP, tile), 1) - lax.broadcasted_iota(
        jnp.int32, (STAMP, tile), 0
    )
    pick = jnp.concatenate(
        [
            jnp.where(apart == offset_ref[0, 0, 0, s], 1.0, 0.0).astype(BF16)
            for s in range(slots)
        ],
        axis=0,
    )

    fetch.wait()
    for halo in halos:
        halo.wait_recv()

    ones = jnp.ones((1, 128), jnp.int32)
    has_up = ones * (mx > 0).astype(jnp.int32) > 0
    has_down = ones * (mx < nx - 1).astype(jnp.int32) > 0
    has_left = ones * (my > 0).astype(jnp.int32) > 0
    has_right = ones * (my < ny - 1).astype(jnp.int32) > 0
    low_lanes = lane1 < MARGIN
    high_lanes = lane1 >= 128 - MARGIN
    for c in range(4):
        for g in range(2):
            r0 = 64 * c
            own = slice(128 * g, 128 * (g + 1))
            total = canvas[MARGIN + r0 : MARGIN + r0 + 64, own]
            if g == 0:
                moved = in_sides[1]
                moved = pltpu.roll(moved, 128 - 32 * c, 1) if c else moved
                total = total + jnp.where(low_lanes & has_left, moved, 0.0)
            else:
                moved = in_sides[0]
                moved = pltpu.roll(moved, 96 - 32 * c, 1) if c < 3 else moved
                total = total + jnp.where(high_lanes & has_right, moved, 0.0)
            if c == 0:
                edge = jnp.where(has_up, in_rows[1, :, own], 0.0)
                if g == 0:
                    edge = edge + jnp.where(low_lanes & has_up & has_left, in_corners[3], 0.0)
                else:
                    edge = edge + jnp.where(high_lanes & has_up & has_right, in_corners[2], 0.0)
                total = jnp.concatenate([total[0:32] + edge, total[32:64]], axis=0)
            if c == 3:
                edge = jnp.where(has_down, in_rows[0, :, own], 0.0)
                if g == 0:
                    edge = edge + jnp.where(low_lanes & has_down & has_left, in_corners[1], 0.0)
                else:
                    edge = edge + jnp.where(high_lanes & has_down & has_right, in_corners[0], 0.0)
                total = jnp.concatenate([total[0:32], total[32:64] + edge], axis=0)
            remain[r0 : r0 + 64, own] = image[r0 : r0 + 64, own] - total
    store = pltpu.make_async_copy(remain, residual_hbm.at[0], copy_sems.at[1])
    store.start()

    high, low = split(remain[...])
    strips = jnp.dot(pick, high, preferred_element_type=F32)
    strips = strips + jnp.dot(pick, low, preferred_element_type=F32)
    for j in range(pairs):
        halves = []
        for odd in range(2):
            s = 2 * j + odd
            at_y = offset_ref[1, 0, 0, s]
            turn = jnp.bitwise_and(at_y, 127)
            block = jnp.right_shift(at_y - turn, 7)
            strip = strips[STAMP * s : STAMP * (s + 1)]
            take_one = jnp.where(lane1 >= turn, block, block + 1) >= 1
            value = jnp.where(take_one, strip[:, 128:256], strip[:, 0:128])
            halves.append(
                pltpu.roll(value, jnp.bitwise_and(STAMP * odd + 256 - turn, 127), 1)
            )
        cutout = jnp.where(first_half, halves[0], halves[1])
        own = slice(128 * j, 128 * (j + 1))
        for k in range(3):
            partial[48 + 8 * k : 56 + 8 * k, own] = fold(blurred[k, :, own] * cutout)
    rights = gather_sums(partial[48:72, :])
    weight = weight_ref[0]
    sums[me] = weight * jnp.concatenate([normal, rights, jnp.zeros((7, 128), F32)], axis=0)

    shares = []
    for d in range(1, nb):
        share = pltpu.make_async_remote_copy(
            src_ref=sums.at[me],
            dst_ref=sums.at[me],
            send_sem=sum_send.at[d - 1],
            recv_sem=sum_recv.at[d - 1],
            device_id=peers[d - 1],
            device_id_type=MESH,
        )
        share.start()
        shares.append(share)
    for d in range(1, nb):
        source = lax.rem(me + nb - d, nb)
        pltpu.make_async_remote_copy(
            src_ref=sums.at[source],
            dst_ref=sums.at[source],
            send_sem=sum_send.at[d - 1],
            recv_sem=sum_recv.at[d - 1],
            device_id=peers[d - 1],
            device_id_type=MESH,
        ).wait_recv()
    total = sums[0]
    for e in range(1, nb):
        total = total + sums[e]

    live = lax.broadcasted_iota(jnp.int32, (1, slots), 1) < live_count
    start = flux_vec[0]
    flux = jnp.where(live, start, 0.0)
    entry = [total[n : n + 1, 0:slots] for n in range(9)]
    m01, m02 = entry[1] * flux, entry[2] * flux
    m12 = entry[4] * flux * flux
    m00 = entry[0] + PRIOR
    m11 = entry[3] * flux * flux + PRIOR
    m22 = entry[5] * flux * flux + PRIOR
    v0, v1, v2 = entry[6], entry[7] * flux, entry[8] * flux
    c00 = m11 * m22 - m12 * m12
    c01 = m12 * m02 - m01 * m22
    c02 = m01 * m12 - m11 * m02
    c11 = m00 * m22 - m02 * m02
    c12 = m01 * m02 - m00 * m12
    c22 = m00 * m11 - m01 * m01
    determinant = m00 * c00 + m01 * c01 + m02 * c02
    change = [
        (c00 * v0 + c01 * v1 + c02 * v2) / determinant,
        (c01 * v0 + c11 * v1 + c12 * v2) / determinant,
        (c02 * v0 + c12 * v1 + c22 * v2) / determinant,
    ]
    bases = [start, shift_vec[0, 0], shift_vec[1, 0]]
    for k in range(3):
        refined_ref[k, 0] = jnp.where(live, bases[k] + change[k], 0.0)

    for share in shares:
        share.wait_send()
    for halo in halos:
        halo.wait_send()
    store.wait()


def shards(
    image,
    psf_taps,
    exposure_weight,
    flux_start,
    centre_shift,
    radius,
    ellipticity,
    offsets,
    source_count,
):
    tile = image.shape[1]
    slots = flux_start.shape[2]
    rows = tile + 2 * MARGIN
    width = slots * STAMP
    smem = pl.BlockSpec(memory_space=pltpu.SMEM)
    vmem = pl.BlockSpec(memory_space=pltpu.VMEM)
    hbm = pl.BlockSpec(memory_space=pl.ANY)
    peers = lax.axis_size("be") - 1
    return pl.pallas_call(
        kernel,
        out_shape=(
            jax.ShapeDtypeStruct((3, 1, 1, slots), F32),
            jax.ShapeDtypeStruct(image.shape, F32),
        ),
        in_specs=[hbm] + [smem] * 8 + [vmem] * 2,
        out_specs=(vmem, hbm),
        scratch_shapes=[
            pltpu.VMEM((tile, tile), F32),
            pltpu.VMEM((3 * STAMP, 2 * width), BF16),
            pltpu.VMEM((2, STAMP, width), F32),
            pltpu.VMEM((3, STAMP, width), F32),
            pltpu.VMEM((width, 384), BF16),
            pltpu.VMEM((width, 384), BF16),
            pltpu.VMEM((rows, 384), F32),
            pltpu.VMEM((STAMP, 128), F32),
            pltpu.VMEM((STAMP, 128), F32),
            pltpu.VMEM((2, MARGIN, tile), F32),
            pltpu.VMEM((2, STAMP, 128), F32),
            pltpu.VMEM((4, MARGIN, 128), F32),
            pltpu.VMEM((tile, tile), F32),
            pltpu.VMEM((72, width), F32),
            pltpu.VMEM((peers + 1, 16, 128), F32),
            pltpu.SemaphoreType.DMA((2,)),
            pltpu.SemaphoreType.DMA((8,)),
            pltpu.SemaphoreType.DMA((8,)),
            pltpu.SemaphoreType.DMA((peers,)),
            pltpu.SemaphoreType.DMA((peers,)),
        ],
        compiler_params=pltpu.CompilerParams(collective_id=0, has_side_effects=True),
        name="photometry",
    )(
        image,
        psf_taps,
        exposure_weight,
        flux_start,
        centre_shift,
        radius,
        ellipticity,
        offsets,
        source_count,
        flux_start,
        centre_shift,
    )


def solution(mesh):
    return jax.shard_map(
        shards,
        mesh=mesh,
        in_specs=(
            P("be", "skyx", "skyy"),
            P("be", None, None),
            P("be"),
            P("skyx", "skyy", None),
            P(None, "skyx", "skyy", None),
            P("skyx", "skyy", None),
            P(None, "skyx", "skyy", None),
            P(None, "skyx", "skyy", None),
            P("skyx", "skyy"),
        ),
        out_specs=(P(None, "skyx", "skyy", None), P("be", "skyx", "skyy")),
        check_vma=False,
    )
```

time: 1050 us -> 23.2 us (0.02)
  the two profiles are of different devices: /device:TPU:24 before, /device:TPU:1 now
where the time goes in v1:
time: 23.2 us; the launch traced here: 23 us
  Pallas kernels  18.2 us (78%)
  local copies, waits for them, and re-layouts  2.91 us (13%)
  between operations  1.94 us (8%)
    pallas_call x1, Pallas kernels, shards(): pl.pallas_call(kernel, out_shape=(jax.ShapeDtypeStruct((3, 1, 1, slots),...  18.2 us
    unnamed x4, local copies, waits for them, and re-layouts  2.91 us

profile of v1, /device:TPU:1, one launch (start us, length us, event | category | flops | bytes accessed | tf_op | source)
XLA Modules:
  0.0 23.0 jit_solution(765020973107351625)
XLA Ops:
  1.9 18.2 %photometry.1 = (f32[3,1,1,16]{3,2,1,0:T(1,128)}, f32[1,256,256]{2,1,0:T(8,128)}) custom-call(f32[1,256,256]{2,1,0:T(8,128)} %image_hbm.1, f32[1,2,15]{2,1,0:T(2,128)} %taps_ref.1, f32[1]{0:T(128)S(6)} %copy.13.weight_ref, f32[1,1,16]{2,1,0:T(1,128)} %flux_vec.1, f32[2,1,1,16]{3,2,1,0:T(1,128)} %shift_vec.1, f32[1,1,16]{2,1,0:T(1,128)} %radius_ref.1, ...), custom_call_target="tpu_custom_call" | custom-call | tf_op jit(solution)/shard_map/photometry/pallas_call | solution.py:450
  20.1 0.0 copy-start
  20.1 0.7 %copy-done = f32[3,1,1,16]{3,2,1,0:T(1,128)S(1)} copy-done((f32[3,1,1,16]{3,2,1,0:T(1,128)S(1)}, f32[3,1,1,16]{3,2,1,0:T(1,128)}, u32[]{:S(2)}) %copy-start) | copy-done | bytes 216
  20.8 0.6 %copy.15 = f32[3,1,1,16]{3,2,1,0:T(1,128)} copy(f32[3,1,1,16]{3,2,1,0:T(1,128)S(1)} %copy-done) | data formatting | bytes 384
  21.4 1.7 %copy.16 = f32[1,256,256]{2,1,0:T(8,128)} copy(f32[1,256,256]{2,1,0:T(8,128)} %get-tuple-element.5) | data formatting | bytes 524288
Async XLA Ops:
  20.1 0.7 %copy-start = (f32[3,1,1,16]{3,2,1,0:T(1,128)S(1)}, f32[3,1,1,16]{3,2,1,0:T(1,128)}, u32[]{:S(2)}) copy-start(f32[3,1,1,16]{3,2,1,0:T(1,128)} %get-tuple-element.4) | copy-start | bytes 580

commit v2 on v1

--- a/solution.py
+++ b/solution.py
@@ -31,6 +31,16 @@
 
 def kernel(
     image_hbm,
+    taps_hbm,
+    weight_hbm,
+    flux_hbm,
+    shift_hbm,
+    radius_hbm,
+    ellipse_hbm,
+    offset_hbm,
+    count_hbm,
+    sums_ref,
+    remain_ref,
     taps_ref,
     weight_ref,
     flux_ref,
@@ -41,8 +51,6 @@
     count_ref,
     flux_vec,
     shift_vec,
-    refined_ref,
-    residual_hbm,
     image,
     stacked,
     field,
@@ -50,12 +58,11 @@
     lanes_high,
     lanes_low,
     canvas,
-    pack_left,
-    pack_right,
+    pack_sides,
+    pack_corners,
     in_rows,
     in_sides,
     in_corners,
-    remain,
     partial,
     sums,
     copy_sems,
@@ -64,7 +71,7 @@
     sum_send,
     sum_recv,
 ):
-    slots = flux_ref.shape[2]
+    slots = flux_hbm.shape[2]
     tile = image_hbm.shape[1]
     pairs = slots // 2
     mx = lax.axis_index("skyx")
@@ -73,25 +80,61 @@
     nx = lax.axis_size("skyx")
     ny = lax.axis_size("skyy")
     nb = lax.axis_size("be")
-    up, down = lax.rem(mx + nx - 1, nx), lax.rem(mx + 1, nx)
-    left, right = lax.rem(my + ny - 1, ny), lax.rem(my + 1, ny)
+    above, below = (mx > 0).astype(jnp.int32), (mx < nx - 1).astype(jnp.int32)
+    before, after = (my > 0).astype(jnp.int32), (my < ny - 1).astype(jnp.int32)
     around = [
-        (up, my, me),
-        (down, my, me),
-        (mx, left, me),
-        (mx, right, me),
-        (up, left, me),
-        (up, right, me),
-        (down, left, me),
-        (down, right, me),
+        (mx - above, my, me),
+        (mx + below, my, me),
+        (mx, my - before, me),
+        (mx, my + after, me),
+        (mx - above, my - before, me),
+        (mx - above, my + after, me),
+        (mx + below, my - before, me),
+        (mx + below, my + after, me),
+    ]
+    exists = [
+        above,
+        below,
+        before,
+        after,
+        above * before,
+        above * after,
+        below * before,
+        below * after,
     ]
     peers = [(mx, my, lax.rem(me + d, nb)) for d in range(1, nb)]
 
     barrier = pltpu.get_barrier_semaphore()
-    for device in around + peers:
+    for device in peers:
         pl.semaphore_signal(barrier, inc=1, device_id=device, device_id_type=MESH)
-    fetch = pltpu.make_async_copy(image_hbm.at[0], image, copy_sems.at[0])
-    fetch.start()
+    for device, there in zip(around, exists):
+
+        @pl.when(there == 1)
+        def _():
+            pl.semaphore_signal(barrier, inc=1, device_id=device, device_id_type=MESH)
+
+    small = [
+        (offset_hbm, offset_ref),
+        (shift_hbm, shift_ref),
+        (radius_hbm, radius_ref),
+        (ellipse_hbm, ellipse_ref),
+        (taps_hbm, taps_ref),
+        (flux_hbm, flux_ref),
+        (count_hbm, count_ref),
+        (weight_hbm, weight_ref),
+        (flux_hbm, flux_vec),
+        (shift_hbm, shift_vec),
+    ]
+    fetches = [
+        pltpu.make_async_copy(source, target, copy_sems.at[n + 1])
+        for n, (source, target) in enumerate(small)
+    ]
+    for fetch in fetches:
+        fetch.start()
+    fetch_image = pltpu.make_async_copy(image_hbm.at[0], image, copy_sems.at[0])
+    fetch_image.start()
+    for fetch in fetches:
+        fetch.wait()
 
     row = lax.broadcasted_iota(jnp.int32, (STAMP, 128), 0)
     lane = lax.broadcasted_iota(jnp.int32, (STAMP, 128), 1)
@@ -179,10 +222,11 @@
         value = pltpu.roll(value, jnp.bitwise_and(turn + 128 - STAMP * odd, 127), 1)
         owner = jnp.where(lane1 >= turn, block, block + 1)
         owner = jnp.where(owner == -1, 2, owner)
+        high, low = split(value)
         for g in range(3):
-            high, low = split(jnp.where(owner == g, value, 0.0))
-            lanes_high[STAMP * s : STAMP * (s + 1), 128 * g : 128 * (g + 1)] = high
-            lanes_low[STAMP * s : STAMP * (s + 1), 128 * g : 128 * (g + 1)] = low
+            keep = jnp.where(owner == g, 1.0, 0.0).astype(BF16)
+            lanes_high[STAMP * s : STAMP * (s + 1), 128 * g : 128 * (g + 1)] = high * keep
+            lanes_low[STAMP * s : STAMP * (s + 1), 128 * g : 128 * (g + 1)] = low * keep
     for j in range(pairs):
         targets.append(pair_of(offset_ref, 0, 0, 0)(j) + column1 + MARGIN)
     target = jnp.concatenate(targets, axis=1)
@@ -193,41 +237,32 @@
     placed = jnp.dot(place, lanes_high[...], preferred_element_type=F32)
     placed = placed + jnp.dot(place, lanes_low[...], preferred_element_type=F32)
     canvas[...] = placed
-    side = placed[MARGIN : MARGIN + tile, 256:384]
-    to_left, to_right = None, None
-    for c in range(4):
-        chunk = side[64 * c : 64 * (c + 1)]
-        here = (lane >= 32 * c) & (lane < 32 * (c + 1))
-        moved = pltpu.roll(chunk, (32 * c + 128 - 96) % 128, 1)
-        to_left = moved if c == 0 else jnp.where(here, moved, to_left)
-        moved = pltpu.roll(chunk, 32 * c, 1) if c else chunk
-        to_right = moved if c == 0 else jnp.where(here, moved, to_right)
-    pack_left[...] = to_left
-    pack_right[...] = to_right
-
-    top = canvas.at[0:MARGIN]
-    bottom = canvas.at[tile + MARGIN : tile + 2 * MARGIN]
-    sources = [
-        top.at[:, 0:tile],
-        bottom.at[:, 0:tile],
-        pack_left,
-        pack_right,
-        top.at[:, tile : tile + 128],
-        top.at[:, tile : tile + 128],
-        bottom.at[:, tile : tile + 128],
-        bottom.at[:, tile : tile + 128],
-    ]
-    landings = [
-        in_rows.at[0],
-        in_rows.at[1],
-        in_sides.at[0],
-        in_sides.at[1],
-        in_corners.at[0],
-        in_corners.at[1],
-        in_corners.at[2],
-        in_corners.at[3],
-    ]
-    pl.semaphore_wait(barrier, len(around) + len(peers))
+
+    def pack(strip, first_lane):
+        size = strip.shape[0] // 4
+        place_in = lax.broadcasted_iota(jnp.int32, (size, 128), 1)
+        out = None
+        for c in range(4):
+            turn = (32 * c + 128 - first_lane) % 128
+            block = strip[size * c : size * (c + 1)]
+            block = pltpu.roll(block, turn, 1) if turn else block
+            out = block if c == 0 else jnp.where(place_in >= 32 * c, block, out)
+        return out
+
+    side = placed[:, tile : tile + 128]
+    bands = [side[MARGIN : MARGIN + tile], side[0:MARGIN], side[MARGIN + tile :]]
+    pack_sides[0] = pack(bands[0], 96)
+    pack_sides[1] = pack(bands[0], 0)
+    pack_corners[0] = pack(bands[1], 96)
+    pack_corners[1] = pack(bands[1], 0)
+    pack_corners[2] = pack(bands[2], 96)
+    pack_corners[3] = pack(bands[2], 0)
+
+    sources = [canvas.at[0:MARGIN, 0:tile], canvas.at[tile + MARGIN :, 0:tile]]
+    sources += [pack_sides.at[d] for d in range(2)] + [pack_corners.at[d] for d in range(4)]
+    landings = [in_rows.at[d] for d in range(2)] + [in_sides.at[d] for d in range(2)]
+    landings += [in_corners.at[d] for d in range(4)]
+    pl.semaphore_wait(barrier, len(peers) + sum(exists))
     halos = [
         pltpu.make_async_remote_copy(
             src_ref=sources[d],
@@ -239,8 +274,11 @@
         )
         for d in range(8)
     ]
-    for halo in halos:
-        halo.start()
+    for halo, there in zip(halos, exists):
+
+        @pl.when(there == 1)
+        def _():
+            halo.start()
 
     for k in range(2):
         for j in range(pairs):
@@ -303,49 +341,56 @@
         axis=0,
     )
 
-    fetch.wait()
-    for halo in halos:
-        halo.wait_recv()
+    fetch_image.wait()
+    opposite = [1, 0, 3, 2, 7, 6, 5, 4]
+    for d in range(8):
+
+        @pl.when(exists[opposite[d]] == 1)
+        def _():
+            halos[d].wait_recv()
 
     ones = jnp.ones((1, 128), jnp.int32)
-    has_up = ones * (mx > 0).astype(jnp.int32) > 0
-    has_down = ones * (mx < nx - 1).astype(jnp.int32) > 0
-    has_left = ones * (my > 0).astype(jnp.int32) > 0
-    has_right = ones * (my < ny - 1).astype(jnp.int32) > 0
+    has_up, has_down, has_left, has_right = [
+        ones * there > 0 for there in (above, below, before, after)
+    ]
     low_lanes = lane1 < MARGIN
     high_lanes = lane1 >= 128 - MARGIN
+
+    def unpack(block, c, first_lane):
+        turn = (first_lane + 128 - 32 * c) % 128
+        return pltpu.roll(block, turn, 1) if turn else block
+
+    def unpack_corner(block, first_lane):
+        return jnp.concatenate([unpack(block, c, first_lane) for c in range(4)], axis=0)
+
     for c in range(4):
         for g in range(2):
             r0 = 64 * c
             own = slice(128 * g, 128 * (g + 1))
             total = canvas[MARGIN + r0 : MARGIN + r0 + 64, own]
             if g == 0:
-                moved = in_sides[1]
-                moved = pltpu.roll(moved, 128 - 32 * c, 1) if c else moved
-                total = total + jnp.where(low_lanes & has_left, moved, 0.0)
+                total = total + jnp.where(low_lanes & has_left, unpack(in_sides[1], c, 0), 0.0)
             else:
-                moved = in_sides[0]
-                moved = pltpu.roll(moved, 96 - 32 * c, 1) if c < 3 else moved
-                total = total + jnp.where(high_lanes & has_right, moved, 0.0)
+                total = total + jnp.where(high_lanes & has_right, unpack(in_sides[0], c, 96), 0.0)
             if c == 0:
                 edge = jnp.where(has_up, in_rows[1, :, own], 0.0)
                 if g == 0:
-                    edge = edge + jnp.where(low_lanes & has_up & has_left, in_corners[3], 0.0)
+                    corner, there = unpack_corner(in_corners[3], 0), low_lanes & has_up & has_left
                 else:
-                    edge = edge + jnp.where(high_lanes & has_up & has_right, in_corners[2], 0.0)
+                    corner, there = unpack_corner(in_corners[2], 96), high_lanes & has_up & has_right
+                edge = edge + jnp.where(there, corner, 0.0)
                 total = jnp.concatenate([total[0:32] + edge, total[32:64]], axis=0)
             if c == 3:
                 edge = jnp.where(has_down, in_rows[0, :, own], 0.0)
                 if g == 0:
-                    edge = edge + jnp.where(low_lanes & has_down & has_left, in_corners[1], 0.0)
+                    corner, there = unpack_corner(in_corners[1], 0), low_lanes & has_down & has_left
                 else:
-                    edge = edge + jnp.where(high_lanes & has_down & has_right, in_corners[0], 0.0)
+                    corner, there = unpack_corner(in_corners[0], 96), high_lanes & has_down & has_right
+                edge = edge + jnp.where(there, corner, 0.0)
                 total = jnp.concatenate([total[0:32], total[32:64] + edge], axis=0)
-            remain[r0 : r0 + 64, own] = image[r0 : r0 + 64, own] - total
-    store = pltpu.make_async_copy(remain, residual_hbm.at[0], copy_sems.at[1])
-    store.start()
-
-    high, low = split(remain[...])
+            remain_ref[0, r0 : r0 + 64, own] = image[r0 : r0 + 64, own] - total
+
+    high, low = split(remain_ref[0])
     strips = jnp.dot(pick, high, preferred_element_type=F32)
     strips = strips + jnp.dot(pick, low, preferred_element_type=F32)
     for j in range(pairs):
@@ -394,11 +439,28 @@
     total = sums[0]
     for e in range(1, nb):
         total = total + sums[e]
-
-    live = lax.broadcasted_iota(jnp.int32, (1, slots), 1) < live_count
-    start = flux_vec[0]
-    flux = jnp.where(live, start, 0.0)
-    entry = [total[n : n + 1, 0:slots] for n in range(9)]
+    sums_ref[...] = total
+    sums_ref[9:10, 0:slots] = flux_vec[0]
+    sums_ref[10:11, 0:slots] = shift_vec[0, 0]
+    sums_ref[11:12, 0:slots] = shift_vec[1, 0]
+    sums_ref[12:13, :] = jnp.where(lane1 < live_count, 1.0, 0.0)
+
+    for share in shares:
+        share.wait_send()
+    for halo, there in zip(halos, exists):
+
+        @pl.when(there == 1)
+        def _():
+            halo.wait_send()
+
+
+def finish(sums_ref, remain_ref, refined_hbm, residual_hbm, refined, sems):
+    store = pltpu.make_async_copy(remain_ref, residual_hbm, sems.at[0])
+    store.start()
+    slots = refined.shape[3]
+    entry = [sums_ref[n : n + 1, 0:slots] for n in range(13)]
+    start, live = entry[9], entry[12]
+    flux = start * live
     m01, m02 = entry[1] * flux, entry[2] * flux
     m12 = entry[4] * flux * flux
     m00 = entry[0] + PRIOR
@@ -417,15 +479,12 @@
         (c01 * v0 + c11 * v1 + c12 * v2) / determinant,
         (c02 * v0 + c12 * v1 + c22 * v2) / determinant,
     ]
-    bases = [start, shift_vec[0, 0], shift_vec[1, 0]]
     for k in range(3):
-        refined_ref[k, 0] = jnp.where(live, bases[k] + change[k], 0.0)
-
-    for share in shares:
-        share.wait_send()
-    for halo in halos:
-        halo.wait_send()
+        refined[k, 0] = (entry[9 + k] + change[k]) * live
+    write = pltpu.make_async_copy(refined, refined_hbm, sems.at[1])
+    write.start()
     store.wait()
+    write.wait()
 
 
 def shards(
@@ -443,44 +502,10 @@
     slots = flux_start.shape[2]
     rows = tile + 2 * MARGIN
     width = slots * STAMP
-    smem = pl.BlockSpec(memory_space=pltpu.SMEM)
     vmem = pl.BlockSpec(memory_space=pltpu.VMEM)
     hbm = pl.BlockSpec(memory_space=pl.ANY)
     peers = lax.axis_size("be") - 1
-    return pl.pallas_call(
-        kernel,
-        out_shape=(
-            jax.ShapeDtypeStruct((3, 1, 1, slots), F32),
-            jax.ShapeDtypeStruct(image.shape, F32),
-        ),
-        in_specs=[hbm] + [smem] * 8 + [vmem] * 2,
-        out_specs=(vmem, hbm),
-        scratch_shapes=[
-            pltpu.VMEM((tile, tile), F32),
-            pltpu.VMEM((3 * STAMP, 2 * width), BF16),
-            pltpu.VMEM((2, STAMP, width), F32),
-            pltpu.VMEM((3, STAMP, width), F32),
-            pltpu.VMEM((width, 384), BF16),
-            pltpu.VMEM((width, 384), BF16),
-            pltpu.VMEM((rows, 384), F32),
-            pltpu.VMEM((STAMP, 128), F32),
-            pltpu.VMEM((STAMP, 128), F32),
-            pltpu.VMEM((2, MARGIN, tile), F32),
-            pltpu.VMEM((2, STAMP, 128), F32),
-            pltpu.VMEM((4, MARGIN, 128), F32),
-            pltpu.VMEM((tile, tile), F32),
-            pltpu.VMEM((72, width), F32),
-            pltpu.VMEM((peers + 1, 16, 128), F32),
-            pltpu.SemaphoreType.DMA((2,)),
-            pltpu.SemaphoreType.DMA((8,)),
-            pltpu.SemaphoreType.DMA((8,)),
-            pltpu.SemaphoreType.DMA((peers,)),
-            pltpu.SemaphoreType.DMA((peers,)),
-        ],
-        compiler_params=pltpu.CompilerParams(collective_id=0, has_side_effects=True),
-        name="photometry",
-    )(
-        image,
+    operands = (
         psf_taps,
         exposure_weight,
         flux_start,
@@ -489,9 +514,52 @@
         ellipticity,
         offsets,
         source_count,
-        flux_start,
-        centre_shift,
     )
+    sums, remain = pl.pallas_call(
+        kernel,
+        out_shape=(pltpu.VMEM((16, 128), F32), pltpu.VMEM(image.shape, F32)),
+        in_specs=[hbm] * 9,
+        out_specs=(vmem, vmem),
+        scratch_shapes=[pltpu.SMEM(operand.shape, operand.dtype) for operand in operands]
+        + [
+            pltpu.VMEM(flux_start.shape, F32),
+            pltpu.VMEM(centre_shift.shape, F32),
+            pltpu.VMEM((tile, tile), F32),
+            pltpu.VMEM((3 * STAMP, 2 * width), BF16),
+            pltpu.VMEM((2, STAMP, width), F32),
+            pltpu.VMEM((3, STAMP, width), F32),
+            pltpu.VMEM((width, tile + 128), BF16),
+            pltpu.VMEM((width, tile + 128), BF16),
+            pltpu.VMEM((rows, tile + 128), F32),
+            pltpu.VMEM((2, STAMP, 128), F32),
+            pltpu.VMEM((4, 8, 128), F32),
+            pltpu.VMEM((2, MARGIN, tile), F32),
+            pltpu.VMEM((2, STAMP, 128), F32),
+            pltpu.VMEM((4, 8, 128), F32),
+            pltpu.VMEM((72, width), F32),
+            pltpu.VMEM((peers + 1, 16, 128), F32),
+            pltpu.SemaphoreType.DMA((11,)),
+            pltpu.SemaphoreType.DMA((8,)),
+            pltpu.SemaphoreType.DMA((8,)),
+            pltpu.SemaphoreType.DMA((peers,)),
+            pltpu.SemaphoreType.DMA((peers,)),
+        ],
+        compiler_params=pltpu.CompilerParams(collective_id=0, has_side_effects=True),
+        name="photometry",
+    )(image, *operands)
+    sums = pltpu.with_memory_space_constraint(sums, pltpu.VMEM)
+    remain = pltpu.with_memory_space_constraint(remain, pltpu.VMEM)
+    return pl.pallas_call(
+        finish,
+        out_shape=(
+            jax.ShapeDtypeStruct((3, 1, 1, slots), F32),
+            jax.ShapeDtypeStruct(image.shape, F32),
+        ),
+        in_specs=[vmem, vmem],
+        out_specs=(hbm, hbm),
+        scratch_shapes=[pltpu.VMEM((3, 1, 1, slots), F32), pltpu.SemaphoreType.DMA((2,))],
+        name="finish",
+    )(sums, remain)
 
 
 def solution(mesh):

time: 23.2 us -> 17.2 us (0.74)
  the two profiles are of different devices: /device:TPU:1 before, /device:TPU:24 now
where the time goes in v2:
time: 17.2 us; the launch traced here: 17.1 us
  Pallas kernels  15.2 us (88%)
  between operations  1.93 us (11%)
    pallas_call x1, Pallas kernels, shards(): pl.pallas_call(kernel, out_shape=(pltpu.VMEM((16, 128), F32), pltpu.VMEM(...  14.4 us
    pallas_call x1, Pallas kernels, shards(): pl.pallas_call(finish, out_shape=(jax.ShapeDtypeStruct((3, 1, 1, slots),...  0.72 us

profile of v2, /device:TPU:24, one launch (start us, length us, event | category | flops | bytes accessed | tf_op | source)
XLA Modules:
  0.0 17.1 jit_solution(5249054434038242500)
XLA Ops:
  1.9 14.4 %photometry.1 = (f32[16,128]{1,0:T(8,128)S(1)}, f32[1,256,256]{2,1,0:T(8,128)S(1)}) custom-call(f32[1,256,256]{2,1,0:T(8,128)} %image_hbm.1, f32[1,2,15]{2,1,0:T(2,128)} %taps_hbm.1, f32[1]{0:T(128)S(6)} %copy.11.weight_hbm, f32[1,1,16]{2,1,0:T(1,128)} %flux_hbm.1, f32[2,1,1,16]{3,2,1,0:T(1,128)} %shift_hbm.1, f32[1,1,16]{2,1,0:T(1,128)} %radius_hbm.1, ...), custom_call_target="tpu_custom_call" | custom-call | tf_op jit(solution)/shard_map/photometry/pallas_call | solution.py:518
  16.4 0.7 %finish.1 = (f32[3,1,1,16]{3,2,1,0:T(1,128)}, f32[1,256,256]{2,1,0:T(8,128)}) custom-call(f32[16,128]{1,0:T(8,128)S(1)} %get-tuple-element.4.sums_ref, f32[1,256,256]{2,1,0:T(8,128)S(1)} %get-tuple-element.5.remain_ref), custom_call_target="tpu_custom_call" | custom-call | tf_op jit(solution)/shard_map/finish/pallas_call | solution.py:552

commit v3 on v2

--- a/solution.py
+++ b/solution.py
@@ -9,6 +9,7 @@
 MARGIN = 32
 TAPS = 15
 PRIOR = 8.0
+EDGES = 4
 F32 = jnp.float32
 BF16 = jnp.bfloat16
 MESH = pl.DeviceIdType.MESH
@@ -52,17 +53,18 @@
     flux_vec,
     shift_vec,
     image,
-    stacked,
-    field,
-    blurred,
-    lanes_high,
-    lanes_low,
-    canvas,
+    edge_stacked,
+    edge_lanes,
+    edge_rows,
     pack_sides,
     pack_corners,
     in_rows,
     in_sides,
     in_corners,
+    stacked,
+    blurred,
+    lanes,
+    blocks,
     partial,
     sums,
     copy_sems,
@@ -83,44 +85,46 @@
     above, below = (mx > 0).astype(jnp.int32), (mx < nx - 1).astype(jnp.int32)
     before, after = (my > 0).astype(jnp.int32), (my < ny - 1).astype(jnp.int32)
     around = [
-        (mx - above, my, me),
-        (mx + below, my, me),
         (mx, my - before, me),
         (mx, my + after, me),
         (mx - above, my - before, me),
         (mx - above, my + after, me),
         (mx + below, my - before, me),
         (mx + below, my + after, me),
+        (mx - above, my, me),
+        (mx + below, my, me),
     ]
     exists = [
-        above,
-        below,
         before,
         after,
         above * before,
         above * after,
         below * before,
         below * after,
+        above,
+        below,
     ]
+    opposite = [1, 0, 5, 4, 3, 2, 7, 6]
     peers = [(mx, my, lax.rem(me + d, nb)) for d in range(1, nb)]
 
     barrier = pltpu.get_barrier_semaphore()
-    for device in peers:
-        pl.semaphore_signal(barrier, inc=1, device_id=device, device_id_type=MESH)
     for device, there in zip(around, exists):
 
         @pl.when(there == 1)
         def _():
             pl.semaphore_signal(barrier, inc=1, device_id=device, device_id_type=MESH)
 
+    for device in peers:
+        pl.semaphore_signal(barrier, inc=1, device_id=device, device_id_type=MESH)
+
     small = [
         (offset_hbm, offset_ref),
+        (count_hbm, count_ref),
         (shift_hbm, shift_ref),
         (radius_hbm, radius_ref),
         (ellipse_hbm, ellipse_ref),
+        (flux_hbm, flux_ref),
         (taps_hbm, taps_ref),
-        (flux_hbm, flux_ref),
-        (count_hbm, count_ref),
         (weight_hbm, weight_ref),
         (flux_hbm, flux_vec),
         (shift_hbm, shift_vec),
@@ -139,15 +143,15 @@
     row = lax.broadcasted_iota(jnp.int32, (STAMP, 128), 0)
     lane = lax.broadcasted_iota(jnp.int32, (STAMP, 128), 1)
     lane1 = lax.broadcasted_iota(jnp.int32, (1, 128), 1)
+    lane16 = lax.broadcasted_iota(jnp.int32, (16, 128), 1)
     first_half = lane1 < STAMP
     column1 = jnp.where(first_half, lane1, lane1 - STAMP)
+    grid_u = row.astype(F32)
+    grid_v = column1.astype(F32)
     live_count = count_ref[0, 0]
 
-    def pair_of(ref, *index):
-        def at(j):
-            return jnp.where(first_half, ref[index + (2 * j,)], ref[index + (2 * j + 1,)])
-
-        return at
+    def pair_of(j, ref, *index):
+        return jnp.where(first_half, ref[index + (2 * j,)], ref[index + (2 * j + 1,)])
 
     rows_band = band(taps_ref, 0, row[:, :STAMP] - lane[:, :STAMP])
     rows_high, rows_low = split(rows_band)
@@ -166,9 +170,8 @@
     )
     right_high, right_low = split(right_factor)
 
-    def blur(count):
-        width = count * slots * STAMP
-        along = jnp.dot(left_factor, stacked[:, :width], preferred_element_type=F32)
+    def blur(ref, width):
+        along = jnp.dot(left_factor, ref[:, :width], preferred_element_type=F32)
         groups = jnp.concatenate(
             [along[:, 256 * g : 256 * (g + 1)] for g in range(width // 256)], axis=0
         )
@@ -177,66 +180,89 @@
         out = out + jnp.dot(low, right_high, preferred_element_type=F32)
         return out + jnp.dot(high, right_low, preferred_element_type=F32)
 
-    def stack(value, start):
+    def stack(ref, value, start):
         high, low = split(value)
-        stacked[0:STAMP, start : start + 128] = high
-        stacked[STAMP : 2 * STAMP, start : start + 128] = low
-        stacked[2 * STAMP : 3 * STAMP, start : start + 128] = high
-
-    grid_u = row.astype(F32)
-    for j in range(pairs):
-        shift_x = pair_of(shift_ref, 0, 0, 0)(j)
-        shift_y = pair_of(shift_ref, 1, 0, 0)(j)
-        radius = pair_of(radius_ref, 0, 0)(j)
-        one = pair_of(ellipse_ref, 0, 0, 0)(j)
-        two = pair_of(ellipse_ref, 1, 0, 0)(j)
+        ref[0:STAMP, start : start + 128] = high
+        ref[STAMP : 2 * STAMP, start : start + 128] = low
+        ref[2 * STAMP : 3 * STAMP, start : start + 128] = high
+
+    def shape(shift_x, shift_y, radius, one, two):
         inverse = 1.0 / (radius * radius)
         coef_a = (1.0 + one) * inverse
         coef_b = two * inverse
         coef_c = (1.0 - one) * inverse
         u = grid_u - (float(STAMP // 2) + shift_x)
-        v = column1.astype(F32) - (float(STAMP // 2) + shift_y)
+        v = grid_v - (float(STAMP // 2) + shift_y)
         along_x = coef_a * u + coef_b * v
         along_y = coef_b * u + coef_c * v
         square = u * along_x + v * along_y + 0.25
         inverse_root = lax.rsqrt(square)
         profile = jnp.exp(-(square * inverse_root))
-        stack(profile, 128 * j)
-        scaled = profile * inverse_root
-        field[0, :, 128 * j : 128 * (j + 1)] = scaled * along_x
-        field[1, :, 128 * j : 128 * (j + 1)] = scaled * along_y
-
-    spread = blur(1)
-    for g in range(slots * STAMP // 256):
-        blurred[0, :, 256 * g : 256 * (g + 1)] = spread[STAMP * g : STAMP * (g + 1)]
-
-    targets = []
-    for s in range(slots):
-        flux = jnp.where(s < live_count, flux_ref[0, 0, s], 0.0)
-        at_y = offset_ref[1, 0, 0, s]
+        return profile, profile * inverse_root, along_x, along_y
+
+    def lane_place(both, odd, at_y, groups, write):
         turn = jnp.bitwise_and(at_y, 127)
         block = jnp.right_shift(at_y - turn, 7)
-        j, odd = s // 2, s % 2
-        value = blurred[0, :, 128 * j : 128 * (j + 1)]
-        value = jnp.where(first_half if odd == 0 else ~first_half, value * flux, 0.0)
-        value = pltpu.roll(value, jnp.bitwise_and(turn + 128 - STAMP * odd, 127), 1)
-        owner = jnp.where(lane1 >= turn, block, block + 1)
+        value = pltpu.roll(both, jnp.bitwise_and(turn + 128 - STAMP * odd, 127), 1)
+        high, low = split(value)
+        owner = jnp.where(lane16 >= turn, block, block + 1)
         owner = jnp.where(owner == -1, 2, owner)
-        high, low = split(value)
-        for g in range(3):
+        owner = jnp.where(jnp.bitwise_and(lane16 - turn, 127) < STAMP, owner, 3)
+        for g in range(groups):
             keep = jnp.where(owner == g, 1.0, 0.0).astype(BF16)
-            lanes_high[STAMP * s : STAMP * (s + 1), 128 * g : 128 * (g + 1)] = high * keep
-            lanes_low[STAMP * s : STAMP * (s + 1), 128 * g : 128 * (g + 1)] = low * keep
-    for j in range(pairs):
-        targets.append(pair_of(offset_ref, 0, 0, 0)(j) + column1 + MARGIN)
-    target = jnp.concatenate(targets, axis=1)
-    rows = tile + 2 * MARGIN
-    place = jnp.where(
-        lax.broadcasted_iota(jnp.int32, (rows, slots * STAMP), 0) == target, 1.0, 0.0
-    ).astype(BF16)
-    placed = jnp.dot(place, lanes_high[...], preferred_element_type=F32)
-    placed = placed + jnp.dot(place, lanes_low[...], preferred_element_type=F32)
-    canvas[...] = placed
+            for r in range(0, STAMP, 16):
+                write(g, 0, r, high[r : r + 16] * keep)
+                write(g, 1, r, low[r : r + 16] * keep)
+
+    keys, found = [], jnp.int32(0)
+    edge_y = [jnp.int32(0)] * EDGES
+    last = tile - STAMP
+    for s in range(slots):
+        at_x, at_y = offset_ref[0, 0, 0, s], offset_ref[1, 0, 0, s]
+        reach = jnp.maximum(jnp.maximum(-at_x, at_x - last), jnp.maximum(-at_y, at_y - last))
+        hit = jnp.where(s < live_count, reach, 0) > 0
+        key = jnp.where(hit, found, -1)
+        found = jnp.where(hit, found + 1, found)
+        keys.append(key)
+        edge_y = [jnp.where(key == k, at_y, edge_y[k]) for k in range(EDGES)]
+    edge = []
+    for h in range(EDGES // 2):
+        which = jnp.where(first_half, 2 * h, 2 * h + 1)
+        values = [jnp.full((1, 128), v, F32) for v in (0.0, 0.0, 1.0, 0.0, 0.0, 0.0)]
+        values.append(jnp.zeros((1, 128), jnp.int32))
+        for s in range(slots):
+            here = which == keys[s]
+            new = [
+                shift_ref[0, 0, 0, s],
+                shift_ref[1, 0, 0, s],
+                radius_ref[0, 0, s],
+                ellipse_ref[0, 0, 0, s],
+                ellipse_ref[1, 0, 0, s],
+                flux_ref[0, 0, s],
+                offset_ref[0, 0, 0, s],
+            ]
+            values = [jnp.where(here, n, v) for n, v in zip(new, values)]
+        edge.append(values)
+        stack(edge_stacked, shape(*values[:5])[0], 128 * h)
+    spread = blur(edge_stacked, STAMP * EDGES)
+    for k in range(EDGES):
+        both = spread[:, 128 * (k // 2) : 128 * (k // 2 + 1)] * edge[k // 2][5]
+
+        def write(g, part, r, value):
+            start = 256 * part + 128 * g if g < 2 else 512 + 128 * part
+            edge_lanes[STAMP * k + r : STAMP * k + r + 16, start : start + 128] = value
+
+        lane_place(both, k % 2, edge_y[k], 3, write)
+    edge_target = jnp.concatenate([values[6] + column1 for values in edge], axis=1)
+    at = lax.broadcasted_iota(jnp.int32, (2 * MARGIN, STAMP * EDGES), 0)
+    at = jnp.where(at < MARGIN, at - MARGIN, at - MARGIN + tile)
+    place = jnp.where(at == edge_target, 1.0, 0.0).astype(BF16)
+    outer = jnp.dot(place, edge_lanes[...], preferred_element_type=F32)
+    at = lax.broadcasted_iota(jnp.int32, (tile, STAMP * EDGES), 0)
+    place = jnp.where(at == edge_target, 1.0, 0.0).astype(BF16)
+    side = jnp.dot(place, edge_lanes[:, 512:768], preferred_element_type=F32)
+    side = side[:, 0:128] + side[:, 128:256]
+    corners = outer[:, 512:640] + outer[:, 640:768]
 
     def pack(strip, first_lane):
         size = strip.shape[0] // 4
@@ -249,19 +275,19 @@
             out = block if c == 0 else jnp.where(place_in >= 32 * c, block, out)
         return out
 
-    side = placed[:, tile : tile + 128]
-    bands = [side[MARGIN : MARGIN + tile], side[0:MARGIN], side[MARGIN + tile :]]
-    pack_sides[0] = pack(bands[0], 96)
-    pack_sides[1] = pack(bands[0], 0)
-    pack_corners[0] = pack(bands[1], 96)
-    pack_corners[1] = pack(bands[1], 0)
-    pack_corners[2] = pack(bands[2], 96)
-    pack_corners[3] = pack(bands[2], 0)
-
-    sources = [canvas.at[0:MARGIN, 0:tile], canvas.at[tile + MARGIN :, 0:tile]]
-    sources += [pack_sides.at[d] for d in range(2)] + [pack_corners.at[d] for d in range(4)]
-    landings = [in_rows.at[d] for d in range(2)] + [in_sides.at[d] for d in range(2)]
-    landings += [in_corners.at[d] for d in range(4)]
+    for p in range(2):
+        strip = corners[MARGIN * p : MARGIN * (p + 1)]
+        edge_rows[p] = outer[MARGIN * p : MARGIN * (p + 1), 0:256] + (
+            outer[MARGIN * p : MARGIN * (p + 1), 256:512]
+        )
+        pack_sides[p] = pack(side, 96 - 96 * p)
+        pack_corners[2 * p] = pack(strip, 96)
+        pack_corners[2 * p + 1] = pack(strip, 0)
+
+    sources = [pack_sides.at[d] for d in range(2)] + [pack_corners.at[d] for d in range(4)]
+    sources += [edge_rows.at[d] for d in range(2)]
+    landings = [in_sides.at[d] for d in range(2)] + [in_corners.at[d] for d in range(4)]
+    landings += [in_rows.at[d] for d in range(2)]
     pl.semaphore_wait(barrier, len(peers) + sum(exists))
     halos = [
         pltpu.make_async_remote_copy(
@@ -280,14 +306,44 @@
         def _():
             halo.start()
 
-    for k in range(2):
-        for j in range(pairs):
-            stack(field[k, :, 128 * j : 128 * (j + 1)], 1024 * k + 128 * j)
-    spread = blur(2)
-    for k in range(2):
-        for g in range(4):
-            start = STAMP * (4 * k + g)
-            blurred[1 + k, :, 256 * g : 256 * (g + 1)] = spread[start : start + STAMP]
+    for j in range(pairs):
+        profile, scaled, along_x, along_y = shape(
+            pair_of(j, shift_ref, 0, 0, 0),
+            pair_of(j, shift_ref, 1, 0, 0),
+            pair_of(j, radius_ref, 0, 0),
+            pair_of(j, ellipse_ref, 0, 0, 0),
+            pair_of(j, ellipse_ref, 1, 0, 0),
+        )
+        stack(stacked, profile, 128 * j)
+        stack(stacked, scaled * along_x, STAMP * slots + 128 * j)
+        stack(stacked, scaled * along_y, 2 * STAMP * slots + 128 * j)
+    spread = blur(stacked, 3 * STAMP * slots)
+    quads = slots // 4
+    for k in range(3):
+        for g in range(quads):
+            start = STAMP * (quads * k + g)
+            blurred[k, :, 256 * g : 256 * (g + 1)] = spread[start : start + STAMP]
+
+    targets = []
+    for j in range(pairs):
+        slot = jnp.where(first_half, 2 * j, 2 * j + 1)
+        flux = jnp.where(slot < live_count, pair_of(j, flux_ref, 0, 0), 0.0)
+        both = blurred[0, :, 128 * j : 128 * (j + 1)] * flux
+        for odd in range(2):
+            s = 2 * j + odd
+
+            def write(g, part, r, value):
+                start = 256 * part + 128 * g
+                lanes[STAMP * s + r : STAMP * s + r + 16, start : start + 128] = value
+
+            lane_place(both, odd, offset_ref[1, 0, 0, s], 2, write)
+        targets.append(pair_of(j, offset_ref, 0, 0, 0) + column1)
+    target = jnp.concatenate(targets, axis=1)
+    at = lax.broadcasted_iota(jnp.int32, (tile, slots * STAMP), 0)
+    place = jnp.where(at == target, 1.0, 0.0).astype(BF16)
+    placed = jnp.dot(place, lanes[...], preferred_element_type=F32)
+    fetch_image.wait()
+    remain_ref[0] = image[...] - (placed[:, :256] + placed[:, 256:])
 
     def fold(value):
         total = value[0:8]
@@ -296,8 +352,8 @@
         return total
 
     for j in range(pairs):
-        at_x = row + pair_of(offset_ref, 0, 0, 0)(j)
-        at_y = column1 + pair_of(offset_ref, 1, 0, 0)(j)
+        at_x = row + pair_of(j, offset_ref, 0, 0, 0)
+        at_y = column1 + pair_of(j, offset_ref, 1, 0, 0)
         inside = (at_x >= 0) & (at_x < tile) & (at_y >= 0) & (at_y < tile)
         own = slice(128 * j, 128 * (j + 1))
         masked = [jnp.where(inside, blurred[k, :, own], 0.0) for k in range(3)]
@@ -330,19 +386,11 @@
 
     normal = gather_sums(partial[0:48, :])
 
-    apart = lax.broadcasted_iota(jnp.int32, (STAMP, tile), 1) - lax.broadcasted_iota(
-        jnp.int32, (STAMP, tile), 0
-    )
-    pick = jnp.concatenate(
-        [
-            jnp.where(apart == offset_ref[0, 0, 0, s], 1.0, 0.0).astype(BF16)
-            for s in range(slots)
-        ],
-        axis=0,
-    )
-
-    fetch_image.wait()
-    opposite = [1, 0, 3, 2, 7, 6, 5, 4]
+    for r in range(MARGIN // 8):
+        for g in range(2):
+            blocks[r, g] = jnp.zeros((8, 128), F32)
+            blocks[tile // 8 + MARGIN // 8 + r, g] = jnp.zeros((8, 128), F32)
+
     for d in range(8):
 
         @pl.when(exists[opposite[d]] == 1)
@@ -367,45 +415,48 @@
         for g in range(2):
             r0 = 64 * c
             own = slice(128 * g, 128 * (g + 1))
-            total = canvas[MARGIN + r0 : MARGIN + r0 + 64, own]
             if g == 0:
-                total = total + jnp.where(low_lanes & has_left, unpack(in_sides[1], c, 0), 0.0)
+                total = jnp.where(low_lanes & has_left, unpack(in_sides[1], c, 0), 0.0)
             else:
-                total = total + jnp.where(high_lanes & has_right, unpack(in_sides[0], c, 96), 0.0)
-            if c == 0:
-                edge = jnp.where(has_up, in_rows[1, :, own], 0.0)
-                if g == 0:
-                    corner, there = unpack_corner(in_corners[3], 0), low_lanes & has_up & has_left
+                total = jnp.where(high_lanes & has_right, unpack(in_sides[0], c, 96), 0.0)
+            if c == 0 or c == 3:
+                there = has_up if c == 0 else has_down
+                fringe = jnp.where(there, in_rows[1 if c == 0 else 0, :, own], 0.0)
+                n = (3 if c == 0 else 1) - g
+                corner = unpack_corner(in_corners[n], 96 * g)
+                there = there & ((low_lanes & has_left) if g == 0 else (high_lanes & has_right))
+                fringe = fringe + jnp.where(there, corner, 0.0)
+                if c == 0:
+                    total = jnp.concatenate([total[0:32] + fringe, total[32:64]], axis=0)
                 else:
-                    corner, there = unpack_corner(in_corners[2], 96), high_lanes & has_up & has_right
-                edge = edge + jnp.where(there, corner, 0.0)
-                total = jnp.concatenate([total[0:32] + edge, total[32:64]], axis=0)
-            if c == 3:
-                edge = jnp.where(has_down, in_rows[0, :, own], 0.0)
-                if g == 0:
-                    corner, there = unpack_corner(in_corners[1], 0), low_lanes & has_down & has_left
-                else:
-                    corner, there = unpack_corner(in_corners[0], 96), high_lanes & has_down & has_right
-                edge = edge + jnp.where(there, corner, 0.0)
-                total = jnp.concatenate([total[0:32], total[32:64] + edge], axis=0)
-            remain_ref[0, r0 : r0 + 64, own] = image[r0 : r0 + 64, own] - total
-
-    high, low = split(remain_ref[0])
-    strips = jnp.dot(pick, high, preferred_element_type=F32)
-    strips = strips + jnp.dot(pick, low, preferred_element_type=F32)
+                    total = jnp.concatenate([total[0:32], total[32:64] + fringe], axis=0)
+            value = remain_ref[0, r0 : r0 + 64, own] - total
+            remain_ref[0, r0 : r0 + 64, own] = value
+            for r in range(8):
+                blocks[MARGIN // 8 + 8 * c + r, g] = value[8 * r : 8 * (r + 1)]
+
+    sub = lax.broadcasted_iota(jnp.int32, (STAMP // 8, 8, 128), 1)
     for j in range(pairs):
         halves = []
         for odd in range(2):
             s = 2 * j + odd
+            at_x = jnp.clip(offset_ref[0, 0, 0, s] + MARGIN, 0, tile - 1)
+            step = jnp.bitwise_and(at_x, 7)
+            first = jnp.right_shift(at_x, 3)
             at_y = offset_ref[1, 0, 0, s]
             turn = jnp.bitwise_and(at_y, 127)
             block = jnp.right_shift(at_y - turn, 7)
-            strip = strips[STAMP * s : STAMP * (s + 1)]
             take_one = jnp.where(lane1 >= turn, block, block + 1) >= 1
-            value = jnp.where(take_one, strip[:, 128:256], strip[:, 0:128])
-            halves.append(
-                pltpu.roll(value, jnp.bitwise_and(STAMP * odd + 256 - turn, 127), 1)
+            value = jnp.stack(
+                [
+                    jnp.where(take_one, blocks[first + r, 1], blocks[first + r, 0])
+                    for r in range(STAMP // 8 + 1)
+                ]
             )
+            value = pltpu.roll(value, jnp.bitwise_and(STAMP * odd + 256 - turn, 127), 2)
+            value = pltpu.roll(value, jnp.bitwise_and(8 - step, 7), 1)
+            value = jnp.where(sub < 8 - step, value[:-1], value[1:])
+            halves.append(value.reshape(STAMP, 128))
         cutout = jnp.where(first_half, halves[0], halves[1])
         own = slice(128 * j, 128 * (j + 1))
         for k in range(3):
@@ -525,17 +576,18 @@
             pltpu.VMEM(flux_start.shape, F32),
             pltpu.VMEM(centre_shift.shape, F32),
             pltpu.VMEM((tile, tile), F32),
-            pltpu.VMEM((3 * STAMP, 2 * width), BF16),
-            pltpu.VMEM((2, STAMP, width), F32),
-            pltpu.VMEM((3, STAMP, width), F32),
-            pltpu.VMEM((width, tile + 128), BF16),
-            pltpu.VMEM((width, tile + 128), BF16),
-            pltpu.VMEM((rows, tile + 128), F32),
+            pltpu.VMEM((3 * STAMP, EDGES * STAMP), BF16),
+            pltpu.VMEM((EDGES * STAMP, 768), BF16),
+            pltpu.VMEM((2, MARGIN, tile), F32),
             pltpu.VMEM((2, STAMP, 128), F32),
             pltpu.VMEM((4, 8, 128), F32),
             pltpu.VMEM((2, MARGIN, tile), F32),
             pltpu.VMEM((2, STAMP, 128), F32),
             pltpu.VMEM((4, 8, 128), F32),
+            pltpu.VMEM((3 * STAMP, 3 * width), BF16),
+            pltpu.VMEM((3, STAMP, width), F32),
+            pltpu.VMEM((width, 2 * tile), BF16),
+            pltpu.VMEM((rows // 8, 2, 8, 128), F32),
             pltpu.VMEM((72, width), F32),
             pltpu.VMEM((peers + 1, 16, 128), F32),
             pltpu.SemaphoreType.DMA((11,)),

time: 17.2 us -> 16.5 us (0.959)
  Pallas kernels: 15.2 us -> 14.4 us
    pallas_call x1, Pallas kernels: 14.4 us -> 13.7 us  [shards(): pl.pallas_call(kernel, out_shape=(pltpu.VMEM((16, 128), F32), pltpu.VMEM(...]
where the time goes in v3:
time: 16.5 us; the launch traced here: 16.3 us
  Pallas kernels  14.4 us (87%)
  between operations  1.93 us (12%)
    pallas_call x1, Pallas kernels, shards(): pl.pallas_call(kernel, out_shape=(pltpu.VMEM((16, 128), F32), pltpu.VMEM(...  13.7 us
    pallas_call x1, Pallas kernels, shards(): pl.pallas_call(finish, out_shape=(jax.ShapeDtypeStruct((3, 1, 1, slots),...  0.72 us

profile of v3, /device:TPU:24, one launch (start us, length us, event | category | flops | bytes accessed | tf_op | source)
XLA Modules:
  0.0 16.3 jit_solution(2929169456760396432)
XLA Ops:
  1.9 13.7 %photometry.1 = (f32[16,128]{1,0:T(8,128)S(1)}, f32[1,256,256]{2,1,0:T(8,128)S(1)}) custom-call(f32[1,256,256]{2,1,0:T(8,128)} %image_hbm.1, f32[1,2,15]{2,1,0:T(2,128)} %taps_hbm.1, f32[1]{0:T(128)S(6)} %copy.11.weight_hbm, f32[1,1,16]{2,1,0:T(1,128)} %flux_hbm.1, f32[2,1,1,16]{3,2,1,0:T(1,128)} %shift_hbm.1, f32[1,1,16]{2,1,0:T(1,128)} %radius_hbm.1, ...), custom_call_target="tpu_custom_call" | custom-call | tf_op jit(solution)/shard_map/photometry/pallas_call | solution.py:569
  15.6 0.7 %finish.1 = (f32[3,1,1,16]{3,2,1,0:T(1,128)}, f32[1,256,256]{2,1,0:T(8,128)}) custom-call(f32[16,128]{1,0:T(8,128)S(1)} %get-tuple-element.4.sums_ref, f32[1,256,256]{2,1,0:T(8,128)S(1)} %get-tuple-element.5.remain_ref), custom_call_target="tpu_custom_call" | custom-call | tf_op jit(solution)/shard_map/finish/pallas_call | solution.py:604

commit v4 on v3

--- a/solution.py
+++ b/solution.py
@@ -33,27 +33,24 @@
 def kernel(
     image_hbm,
     taps_hbm,
-    weight_hbm,
+    weight_ref,
     flux_hbm,
     shift_hbm,
     radius_hbm,
     ellipse_hbm,
     offset_hbm,
-    count_hbm,
+    count_ref,
     sums_ref,
     remain_ref,
     taps_ref,
-    weight_ref,
     flux_ref,
     shift_ref,
     radius_ref,
     ellipse_ref,
     offset_ref,
-    count_ref,
     flux_vec,
     shift_vec,
     image,
-    edge_stacked,
     edge_lanes,
     edge_rows,
     pack_sides,
@@ -66,12 +63,15 @@
     lanes,
     blocks,
     partial,
-    sums,
+    normals,
+    rights,
     copy_sems,
     send_sems,
     recv_sems,
-    sum_send,
-    sum_recv,
+    normal_send,
+    normal_recv,
+    right_send,
+    right_recv,
 ):
     slots = flux_hbm.shape[2]
     tile = image_hbm.shape[1]
@@ -114,30 +114,26 @@
         def _():
             pl.semaphore_signal(barrier, inc=1, device_id=device, device_id_type=MESH)
 
-    for device in peers:
-        pl.semaphore_signal(barrier, inc=1, device_id=device, device_id_type=MESH)
-
     small = [
         (offset_hbm, offset_ref),
-        (count_hbm, count_ref),
         (shift_hbm, shift_ref),
         (radius_hbm, radius_ref),
         (ellipse_hbm, ellipse_ref),
         (flux_hbm, flux_ref),
         (taps_hbm, taps_ref),
-        (weight_hbm, weight_ref),
-        (flux_hbm, flux_vec),
-        (shift_hbm, shift_vec),
     ]
+    late = [(image_hbm.at[0], image), (flux_hbm, flux_vec), (shift_hbm, shift_vec)]
     fetches = [
-        pltpu.make_async_copy(source, target, copy_sems.at[n + 1])
-        for n, (source, target) in enumerate(small)
+        pltpu.make_async_copy(source, target, copy_sems.at[n])
+        for n, (source, target) in enumerate(small + late)
     ]
-    for fetch in fetches:
+    for fetch in fetches[: len(small)]:
         fetch.start()
-    fetch_image = pltpu.make_async_copy(image_hbm.at[0], image, copy_sems.at[0])
-    fetch_image.start()
-    for fetch in fetches:
+    for device in peers:
+        pl.semaphore_signal(barrier, inc=1, device_id=device, device_id_type=MESH)
+    for fetch in fetches[len(small) :]:
+        fetch.start()
+    for fetch in fetches[: len(small)]:
         fetch.wait()
 
     row = lax.broadcasted_iota(jnp.int32, (STAMP, 128), 0)
@@ -153,32 +149,41 @@
     def pair_of(j, ref, *index):
         return jnp.where(first_half, ref[index + (2 * j,)], ref[index + (2 * j + 1,)])
 
-    rows_band = band(taps_ref, 0, row[:, :STAMP] - lane[:, :STAMP])
-    rows_high, rows_low = split(rows_band)
+    rows_band = jnp.where(lane < STAMP, band(taps_ref, 0, row - lane), 0.0)
+    columns_band = jnp.where(lane < STAMP, band(taps_ref, 1, lane - row), 0.0)
+    nothing = jnp.zeros((STAMP, 128), F32)
+
+    def diagonal(block):
+        other = pltpu.roll(block, STAMP, 1)
+        return jnp.concatenate(
+            [
+                jnp.concatenate([block, nothing], axis=1),
+                jnp.concatenate([other, nothing], axis=1),
+                jnp.concatenate([nothing, block], axis=1),
+                jnp.concatenate([nothing, other], axis=1),
+            ],
+            axis=0,
+        )
+
+    right_high, right_low = split(diagonal(columns_band))
+    left_high, left_low = split(diagonal(rows_band))
+    rows_high, rows_low = left_high[:STAMP, :STAMP], left_low[:STAMP, :STAMP]
     left_factor = jnp.concatenate([rows_high, rows_high, rows_low], axis=1)
-    columns_band = jnp.where(lane < STAMP, band(taps_ref, 1, lane - row), 0.0)
-    columns_next = pltpu.roll(columns_band, STAMP, 1)
-    nothing = jnp.zeros((STAMP, 128), F32)
-    right_factor = jnp.concatenate(
-        [
-            jnp.concatenate([columns_band, nothing], axis=1),
-            jnp.concatenate([columns_next, nothing], axis=1),
-            jnp.concatenate([nothing, columns_band], axis=1),
-            jnp.concatenate([nothing, columns_next], axis=1),
-        ],
-        axis=0,
-    )
-    right_high, right_low = split(right_factor)
+
+    def blur_columns(groups):
+        size = groups.shape[0]
+        high, low = split(groups)
+        out = jnp.dot(
+            jnp.concatenate([high, low], axis=0), right_high, preferred_element_type=F32
+        )
+        return out[:size] + out[size:] + jnp.dot(high, right_low, preferred_element_type=F32)
 
     def blur(ref, width):
         along = jnp.dot(left_factor, ref[:, :width], preferred_element_type=F32)
         groups = jnp.concatenate(
             [along[:, 256 * g : 256 * (g + 1)] for g in range(width // 256)], axis=0
         )
-        high, low = split(groups)
-        out = jnp.dot(high, right_high, preferred_element_type=F32)
-        out = out + jnp.dot(low, right_high, preferred_element_type=F32)
-        return out + jnp.dot(high, right_low, preferred_element_type=F32)
+        return blur_columns(groups)
 
     def stack(ref, value, start):
         high, low = split(value)
@@ -225,7 +230,7 @@
         found = jnp.where(hit, found + 1, found)
         keys.append(key)
         edge_y = [jnp.where(key == k, at_y, edge_y[k]) for k in range(EDGES)]
-    edge = []
+    edge, edge_profiles = [], []
     for h in range(EDGES // 2):
         which = jnp.where(first_half, 2 * h, 2 * h + 1)
         values = [jnp.full((1, 128), v, F32) for v in (0.0, 0.0, 1.0, 0.0, 0.0, 0.0)]
@@ -243,8 +248,8 @@
             ]
             values = [jnp.where(here, n, v) for n, v in zip(new, values)]
         edge.append(values)
-        stack(edge_stacked, shape(*values[:5])[0], 128 * h)
-    spread = blur(edge_stacked, STAMP * EDGES)
+        edge_profiles.append(shape(*values[:5])[0])
+    spread = blur_columns(jnp.concatenate(edge_profiles, axis=1))
     for k in range(EDGES):
         both = spread[:, 128 * (k // 2) : 128 * (k // 2 + 1)] * edge[k // 2][5]
 
@@ -254,13 +259,24 @@
 
         lane_place(both, k % 2, edge_y[k], 3, write)
     edge_target = jnp.concatenate([values[6] + column1 for values in edge], axis=1)
-    at = lax.broadcasted_iota(jnp.int32, (2 * MARGIN, STAMP * EDGES), 0)
-    at = jnp.where(at < MARGIN, at - MARGIN, at - MARGIN + tile)
+    at = lax.broadcasted_iota(jnp.int32, (tile + 2 * MARGIN, STAMP * EDGES), 0)
+    at = jnp.where(at < 2 * MARGIN, jnp.where(at < MARGIN, at - MARGIN, at - MARGIN + tile), at - 2 * MARGIN)
     place = jnp.where(at == edge_target, 1.0, 0.0).astype(BF16)
-    outer = jnp.dot(place, edge_lanes[...], preferred_element_type=F32)
-    at = lax.broadcasted_iota(jnp.int32, (tile, STAMP * EDGES), 0)
-    place = jnp.where(at == edge_target, 1.0, 0.0).astype(BF16)
-    side = jnp.dot(place, edge_lanes[:, 512:768], preferred_element_type=F32)
+    high = jnp.dot(place, left_high, preferred_element_type=F32).astype(BF16)
+    low = jnp.dot(place, left_low, preferred_element_type=F32).astype(BF16)
+    first = 2 * MARGIN
+    outer = jnp.dot(
+        jnp.concatenate([high[:first], low[:first]], axis=0),
+        edge_lanes[...],
+        preferred_element_type=F32,
+    )
+    outer = outer[:first] + outer[first:]
+    side = jnp.dot(
+        jnp.concatenate([high[first:], low[first:]], axis=0),
+        edge_lanes[:, 512:768],
+        preferred_element_type=F32,
+    )
+    side = side[:tile] + side[tile:]
     side = side[:, 0:128] + side[:, 128:256]
     corners = outer[:, 512:640] + outer[:, 640:768]
 
@@ -342,7 +358,8 @@
     at = lax.broadcasted_iota(jnp.int32, (tile, slots * STAMP), 0)
     place = jnp.where(at == target, 1.0, 0.0).astype(BF16)
     placed = jnp.dot(place, lanes[...], preferred_element_type=F32)
-    fetch_image.wait()
+    for fetch in fetches[len(small) :]:
+        fetch.wait()
     remain_ref[0] = image[...] - (placed[:, :256] + placed[:, 256:])
 
     def fold(value):
@@ -373,18 +390,36 @@
     ).astype(BF16)
 
     def gather_sums(value):
-        high, low = split(value)
-        out = jnp.dot(high, segment, preferred_element_type=F32)
-        out = out + jnp.dot(low, segment, preferred_element_type=F32)
-        return jnp.concatenate(
-            [
-                jnp.sum(out[8 * k : 8 * (k + 1)], axis=0, keepdims=True)
-                for k in range(value.shape[0] // 8)
-            ],
-            axis=0,
+        size = value.shape[0]
+        out = jnp.dot(
+            jnp.concatenate(split(value), axis=0), segment, preferred_element_type=F32
         )
-
+        out = out[:size] + out[size:]
+        return [
+            jnp.sum(out[8 * k : 8 * (k + 1)], axis=0, keepdims=True) for k in range(size // 8)
+        ]
+
+    def shares_of(ref, send, recv):
+        def share(slot, d):
+            return pltpu.make_async_remote_copy(
+                src_ref=ref.at[slot],
+                dst_ref=ref.at[slot],
+                send_sem=send.at[d - 1],
+                recv_sem=recv.at[d - 1],
+                device_id=peers[d - 1],
+                device_id_type=MESH,
+            )
+
+        order = sorted(range(1, nb), key=lambda d: -min(d, nb - d))
+        sent = [share(me, d) for d in order]
+        for copy in sent:
+            copy.start()
+        return sent, [(share, lax.rem(me + nb - d, nb), d) for d in order]
+
+    weight = weight_ref[0]
     normal = gather_sums(partial[0:48, :])
+    normals[me] = weight * jnp.concatenate(normal + [jnp.zeros((2, 128), F32)], axis=0)
+    sent, expected = shares_of(normals, normal_send, normal_recv)
 
     for r in range(MARGIN // 8):
         for g in range(2):
@@ -461,42 +496,28 @@
         own = slice(128 * j, 128 * (j + 1))
         for k in range(3):
             partial[48 + 8 * k : 56 + 8 * k, own] = fold(blurred[k, :, own] * cutout)
-    rights = gather_sums(partial[48:72, :])
-    weight = weight_ref[0]
-    sums[me] = weight * jnp.concatenate([normal, rights, jnp.zeros((7, 128), F32)], axis=0)
-
-    shares = []
-    for d in range(1, nb):
-        share = pltpu.make_async_remote_copy(
-            src_ref=sums.at[me],
-            dst_ref=sums.at[me],
-            send_sem=sum_send.at[d - 1],
-            recv_sem=sum_recv.at[d - 1],
-            device_id=peers[d - 1],
-            device_id_type=MESH,
-        )
-        share.start()
-        shares.append(share)
-    for d in range(1, nb):
-        source = lax.rem(me + nb - d, nb)
-        pltpu.make_async_remote_copy(
-            src_ref=sums.at[source],
-            dst_ref=sums.at[source],
-            send_sem=sum_send.at[d - 1],
-            recv_sem=sum_recv.at[d - 1],
-            device_id=peers[d - 1],
-            device_id_type=MESH,
-        ).wait_recv()
-    total = sums[0]
+    right = gather_sums(partial[48:72, :])
+    right = right[0] + pltpu.roll(right[1], slots, 1) + pltpu.roll(right[2], 2 * slots, 1)
+    rights[me] = weight * right
+    more, others = shares_of(rights, right_send, right_recv)
+    for share, slot, d in expected:
+        share(slot, d).wait_recv()
+    total = normals[0]
     for e in range(1, nb):
-        total = total + sums[e]
-    sums_ref[...] = total
+        total = total + normals[e]
+    sums_ref[0:8] = total
+    for share, slot, d in others:
+        share(slot, d).wait_recv()
+    total = rights[0]
+    for e in range(1, nb):
+        total = total + rights[e]
+    sums_ref[8:9] = total
     sums_ref[9:10, 0:slots] = flux_vec[0]
     sums_ref[10:11, 0:slots] = shift_vec[0, 0]
     sums_ref[11:12, 0:slots] = shift_vec[1, 0]
     sums_ref[12:13, :] = jnp.where(lane1 < live_count, 1.0, 0.0)
 
-    for share in shares:
+    for share in sent + more:
         share.wait_send()
     for halo, there in zip(halos, exists):
 
@@ -517,7 +538,8 @@
     m00 = entry[0] + PRIOR
     m11 = entry[3] * flux * flux + PRIOR
     m22 = entry[5] * flux * flux + PRIOR
-    v0, v1, v2 = entry[6], entry[7] * flux, entry[8] * flux
+    right = [sums_ref[8:9, slots * k : slots * (k + 1)] for k in range(3)]
+    v0, v1, v2 = right[0], right[1] * flux, right[2] * flux
     c00 = m11 * m22 - m12 * m12
     c01 = m12 * m02 - m01 * m22
     c02 = m01 * m12 - m11 * m02
@@ -556,27 +578,18 @@
     vmem = pl.BlockSpec(memory_space=pltpu.VMEM)
     hbm = pl.BlockSpec(memory_space=pl.ANY)
     peers = lax.axis_size("be") - 1
-    operands = (
-        psf_taps,
-        exposure_weight,
-        flux_start,
-        centre_shift,
-        radius,
-        ellipticity,
-        offsets,
-        source_count,
-    )
+    smem = pl.BlockSpec(memory_space=pltpu.SMEM)
+    fetched = (psf_taps, flux_start, centre_shift, radius, ellipticity, offsets)
     sums, remain = pl.pallas_call(
         kernel,
         out_shape=(pltpu.VMEM((16, 128), F32), pltpu.VMEM(image.shape, F32)),
-        in_specs=[hbm] * 9,
+        in_specs=[hbm] * 2 + [smem] + [hbm] * 5 + [smem],
         out_specs=(vmem, vmem),
-        scratch_shapes=[pltpu.SMEM(operand.shape, operand.dtype) for operand in operands]
+        scratch_shapes=[pltpu.SMEM(operand.shape, operand.dtype) for operand in fetched]
         + [
             pltpu.VMEM(flux_start.shape, F32),
             pltpu.VMEM(centre_shift.shape, F32),
             pltpu.VMEM((tile, tile), F32),
-            pltpu.VMEM((3 * STAMP, EDGES * STAMP), BF16),
             pltpu.VMEM((EDGES * STAMP, 768), BF16),
             pltpu.VMEM((2, MARGIN, tile), F32),
             pltpu.VMEM((2, STAMP, 128), F32),
@@ -589,16 +602,29 @@
             pltpu.VMEM((width, 2 * tile), BF16),
             pltpu.VMEM((rows // 8, 2, 8, 128), F32),
             pltpu.VMEM((72, width), F32),
-            pltpu.VMEM((peers + 1, 16, 128), F32),
-            pltpu.SemaphoreType.DMA((11,)),
+            pltpu.VMEM((peers + 1, 8, 128), F32),
+            pltpu.VMEM((peers + 1, 1, 128), F32),
+            pltpu.SemaphoreType.DMA((9,)),
             pltpu.SemaphoreType.DMA((8,)),
             pltpu.SemaphoreType.DMA((8,)),
+            pltpu.SemaphoreType.DMA((peers,)),
+            pltpu.SemaphoreType.DMA((peers,)),
             pltpu.SemaphoreType.DMA((peers,)),
             pltpu.SemaphoreType.DMA((peers,)),
         ],
         compiler_params=pltpu.CompilerParams(collective_id=0, has_side_effects=True),
         name="photometry",
-    )(image, *operands)
+    )(
+        image,
+        psf_taps,
+        exposure_weight,
+        flux_start,
+        centre_shift,
+        radius,
+        ellipticity,
+        offsets,
+        source_count,
+    )
     sums = pltpu.with_memory_space_constraint(sums, pltpu.VMEM)
     remain = pltpu.with_memory_space_constraint(remain, pltpu.VMEM)
     return pl.pallas_call(

time: 16.5 us -> 16.3 us (0.988)
  Pallas kernels: 14.4 us -> 14.2 us
    pallas_call x1, Pallas kernels: 13.7 us -> 13.5 us  [shards(): pl.pallas_call(kernel, out_shape=(pltpu.VMEM((16, 128), F32), pltpu.VMEM(...]
where the time goes in v4:
time: 16.3 us; the launch traced here: 16.2 us
  Pallas kernels  14.2 us (87%)
  between operations  1.93 us (12%)
    pallas_call x1, Pallas kernels, shards(): pl.pallas_call(kernel, out_shape=(pltpu.VMEM((16, 128), F32), pltpu.VMEM(...  13.5 us
    pallas_call x1, Pallas kernels, shards(): pl.pallas_call(finish, out_shape=(jax.ShapeDtypeStruct((3, 1, 1, slots),...  0.73 us

profile of v4, /device:TPU:24, one launch (start us, length us, event | category | flops | bytes accessed | tf_op | source)
XLA Modules:
  0.0 16.2 jit_solution(15578197883924259534)
XLA Ops:
  1.9 13.5 %photometry.1 = (f32[16,128]{1,0:T(8,128)S(1)}, f32[1,256,256]{2,1,0:T(8,128)S(1)}) custom-call(f32[1,256,256]{2,1,0:T(8,128)} %image_hbm.1, f32[1,2,15]{2,1,0:T(2,128)} %taps_hbm.1, f32[1]{0:T(128)S(6)} %copy.11.weight_ref, f32[1,1,16]{2,1,0:T(1,128)} %flux_hbm.1, f32[2,1,1,16]{3,2,1,0:T(1,128)} %shift_hbm.1, f32[1,1,16]{2,1,0:T(1,128)} %radius_hbm.1, ...), custom_call_target="tpu_custom_call" | custom-call | tf_op jit(solution)/shard_map/photometry/pallas_call | solution.py:583
  15.4 0.7 %finish.1 = (f32[3,1,1,16]{3,2,1,0:T(1,128)}, f32[1,256,256]{2,1,0:T(8,128)}) custom-call(f32[16,128]{1,0:T(8,128)S(1)} %get-tuple-element.4.sums_ref, f32[1,256,256]{2,1,0:T(8,128)S(1)} %get-tuple-element.5.remain_ref), custom_call_target="tpu_custom_call" | custom-call | tf_op jit(solution)/shard_map/finish/pallas_call | solution.py:630

commit v5 on v4

--- a/solution.py
+++ b/solution.py
@@ -108,12 +108,6 @@
     peers = [(mx, my, lax.rem(me + d, nb)) for d in range(1, nb)]
 
     barrier = pltpu.get_barrier_semaphore()
-    for device, there in zip(around, exists):
-
-        @pl.when(there == 1)
-        def _():
-            pl.semaphore_signal(barrier, inc=1, device_id=device, device_id_type=MESH)
-
     small = [
         (offset_hbm, offset_ref),
         (shift_hbm, shift_ref),
@@ -129,6 +123,12 @@
     ]
     for fetch in fetches[: len(small)]:
         fetch.start()
+    for device, there in zip(around, exists):
+
+        @pl.when(there == 1)
+        def _():
+            pl.semaphore_signal(barrier, inc=1, device_id=device, device_id_type=MESH)
+
     for device in peers:
         pl.semaphore_signal(barrier, inc=1, device_id=device, device_id_type=MESH)
     for fetch in fetches[len(small) :]:
@@ -500,60 +500,60 @@
     right = right[0] + pltpu.roll(right[1], slots, 1) + pltpu.roll(right[2], 2 * slots, 1)
     rights[me] = weight * right
     more, others = shares_of(rights, right_send, right_recv)
+
+    for halo, there in zip(halos, exists):
+
+        @pl.when(there == 1)
+        def _():
+            halo.wait_send()
+
+    for share in sent:
+        share.wait_send()
     for share, slot, d in expected:
         share(slot, d).wait_recv()
     total = normals[0]
     for e in range(1, nb):
         total = total + normals[e]
-    sums_ref[0:8] = total
-    for share, slot, d in others:
-        share(slot, d).wait_recv()
-    total = rights[0]
-    for e in range(1, nb):
-        total = total + rights[e]
-    sums_ref[8:9] = total
-    sums_ref[9:10, 0:slots] = flux_vec[0]
-    sums_ref[10:11, 0:slots] = shift_vec[0, 0]
-    sums_ref[11:12, 0:slots] = shift_vec[1, 0]
-    sums_ref[12:13, :] = jnp.where(lane1 < live_count, 1.0, 0.0)
-
-    for share in sent + more:
-        share.wait_send()
-    for halo, there in zip(halos, exists):
-
-        @pl.when(there == 1)
-        def _():
-            halo.wait_send()
-
-
-def finish(sums_ref, remain_ref, refined_hbm, residual_hbm, refined, sems):
-    store = pltpu.make_async_copy(remain_ref, residual_hbm, sems.at[0])
-    store.start()
-    slots = refined.shape[3]
-    entry = [sums_ref[n : n + 1, 0:slots] for n in range(13)]
-    start, live = entry[9], entry[12]
-    flux = start * live
-    m01, m02 = entry[1] * flux, entry[2] * flux
-    m12 = entry[4] * flux * flux
-    m00 = entry[0] + PRIOR
-    m11 = entry[3] * flux * flux + PRIOR
+    entry = [total[n : n + 1, 0:slots] for n in range(6)]
+    live = lax.broadcasted_iota(jnp.int32, (1, slots), 1) < live_count
+    flux = jnp.where(live, flux_vec[0], 0.0)
+    m00, m01, m02 = entry[0] + PRIOR, entry[1] * flux, entry[2] * flux
+    m11, m12 = entry[3] * flux * flux + PRIOR, entry[4] * flux * flux
     m22 = entry[5] * flux * flux + PRIOR
-    right = [sums_ref[8:9, slots * k : slots * (k + 1)] for k in range(3)]
-    v0, v1, v2 = right[0], right[1] * flux, right[2] * flux
     c00 = m11 * m22 - m12 * m12
     c01 = m12 * m02 - m01 * m22
     c02 = m01 * m12 - m11 * m02
     c11 = m00 * m22 - m02 * m02
     c12 = m01 * m02 - m00 * m12
     c22 = m00 * m11 - m01 * m01
-    determinant = m00 * c00 + m01 * c01 + m02 * c02
-    change = [
-        (c00 * v0 + c01 * v1 + c02 * v2) / determinant,
-        (c01 * v0 + c11 * v1 + c12 * v2) / determinant,
-        (c02 * v0 + c12 * v1 + c22 * v2) / determinant,
-    ]
+    scale = jnp.where(live, 1.0, 0.0) / (m00 * c00 + m01 * c01 + m02 * c02)
+    rows = [c00, c01, c02, c01, c11, c12, c02, c12, c22]
+    for n in range(9):
+        sums_ref[n : n + 1, 0:slots] = rows[n] * (scale if n % 3 == 0 else scale * flux)
+    bases = [flux_vec[0], shift_vec[0, 0], shift_vec[1, 0]]
     for k in range(3):
-        refined[k, 0] = (entry[9 + k] + change[k]) * live
+        sums_ref[9 + k : 10 + k, 0:slots] = jnp.where(live, bases[k], 0.0)
+
+    for share, slot, d in others:
+        share(slot, d).wait_recv()
+    total = rights[0]
+    for e in range(1, nb):
+        total = total + rights[e]
+    sums_ref[12:13] = total
+    for share in more:
+        share.wait_send()
+
+
+def finish(sums_ref, remain_ref, refined_hbm, residual_hbm, refined, sems):
+    store = pltpu.make_async_copy(remain_ref, residual_hbm, sems.at[0])
+    store.start()
+    slots = refined.shape[3]
+    right = [sums_ref[12:13, slots * k : slots * (k + 1)] for k in range(3)]
+    for k in range(3):
+        value = sums_ref[9 + k : 10 + k, 0:slots]
+        for l in range(3):
+            value = value + sums_ref[3 * k + l : 3 * k + l + 1, 0:slots] * right[l]
+        refined[k, 0] = value
     write = pltpu.make_async_copy(refined, refined_hbm, sems.at[1])
     write.start()
     store.wait()

time: 16.3 us -> 16.3 us (level)
  no operation moved by 1% of the time
where the time goes in v5:
time: 16.3 us; the launch traced here: 16.1 us
  Pallas kernels  14.2 us (87%)
  between operations  1.93 us (12%)
    pallas_call x1, Pallas kernels, shards(): pl.pallas_call(kernel, out_shape=(pltpu.VMEM((16, 128), F32), pltpu.VMEM(...  13.5 us
    pallas_call x1, Pallas kernels, shards(): pl.pallas_call(finish, out_shape=(jax.ShapeDtypeStruct((3, 1, 1, slots),...  0.72 us

profile of v5, /device:TPU:24, one launch (start us, length us, event | category | flops | bytes accessed | tf_op | source)
XLA Modules:
  0.0 16.1 jit_solution(6778062127404185337)
XLA Ops:
  1.9 13.5 %photometry.1 = (f32[16,128]{1,0:T(8,128)S(1)}, f32[1,256,256]{2,1,0:T(8,128)S(1)}) custom-call(f32[1,256,256]{2,1,0:T(8,128)} %image_hbm.1, f32[1,2,15]{2,1,0:T(2,128)} %taps_hbm.1, f32[1]{0:T(128)S(6)} %copy.11.weight_ref, f32[1,1,16]{2,1,0:T(1,128)} %flux_hbm.1, f32[2,1,1,16]{3,2,1,0:T(1,128)} %shift_hbm.1, f32[1,1,16]{2,1,0:T(1,128)} %radius_hbm.1, ...), custom_call_target="tpu_custom_call" | custom-call | tf_op jit(solution)/shard_map/photometry/pallas_call | solution.py:583
  15.4 0.7 %finish.1 = (f32[3,1,1,16]{3,2,1,0:T(1,128)}, f32[1,256,256]{2,1,0:T(8,128)}) custom-call(f32[16,128]{1,0:T(8,128)S(1)} %get-tuple-element.4.sums_ref, f32[1,256,256]{2,1,0:T(8,128)S(1)} %get-tuple-element.5.remain_ref), custom_call_target="tpu_custom_call" | custom-call | tf_op jit(solution)/shard_map/finish/pallas_call | solution.py:630

commit v6 on v5

--- a/solution.py
+++ b/solution.py
@@ -62,6 +62,7 @@
     blurred,
     lanes,
     blocks,
+    shifted,
     partial,
     normals,
     rights,
@@ -108,6 +109,12 @@
     peers = [(mx, my, lax.rem(me + d, nb)) for d in range(1, nb)]
 
     barrier = pltpu.get_barrier_semaphore()
+    for device, there in zip(around, exists):
+
+        @pl.when(there == 1)
+        def _():
+            pl.semaphore_signal(barrier, inc=1, device_id=device, device_id_type=MESH)
+
     small = [
         (offset_hbm, offset_ref),
         (shift_hbm, shift_ref),
@@ -123,12 +130,6 @@
     ]
     for fetch in fetches[: len(small)]:
         fetch.start()
-    for device, there in zip(around, exists):
-
-        @pl.when(there == 1)
-        def _():
-            pl.semaphore_signal(barrier, inc=1, device_id=device, device_id_type=MESH)
-
     for device in peers:
         pl.semaphore_signal(barrier, inc=1, device_id=device, device_id_type=MESH)
     for fetch in fetches[len(small) :]:
@@ -368,14 +369,28 @@
             total = total + value[r : r + 8]
         return total
 
+    sub = lax.broadcasted_iota(jnp.int32, (STAMP // 8 + 1, 8, 128), 1)
+    none = jnp.zeros((1, 8, 128), F32)
     for j in range(pairs):
         at_x = row + pair_of(j, offset_ref, 0, 0, 0)
         at_y = column1 + pair_of(j, offset_ref, 1, 0, 0)
         inside = (at_x >= 0) & (at_x < tile) & (at_y >= 0) & (at_y < tile)
         own = slice(128 * j, 128 * (j + 1))
         masked = [jnp.where(inside, blurred[k, :, own], 0.0) for k in range(3)]
+        steps = [jnp.bitwise_and(offset_ref[0, 0, 0, 2 * j + odd], 7) for odd in range(2)]
         for k in range(3):
-            blurred[k, :, own] = masked[k]
+            value = masked[k].reshape(STAMP // 8, 8, 128)
+            moved = []
+            for step in steps:
+                turned = pltpu.roll(value, step, 1)
+                moved.append(
+                    jnp.where(
+                        sub < step,
+                        jnp.concatenate([none, turned], axis=0),
+                        jnp.concatenate([turned, none], axis=0),
+                    )
+                )
+            shifted[k, 9 * j : 9 * (j + 1)] = jnp.where(first_half, moved[0], moved[1])
         n = 0
         for k in range(3):
             for l in range(k, 3):
@@ -470,13 +485,11 @@
             for r in range(8):
                 blocks[MARGIN // 8 + 8 * c + r, g] = value[8 * r : 8 * (r + 1)]
 
-    sub = lax.broadcasted_iota(jnp.int32, (STAMP // 8, 8, 128), 1)
     for j in range(pairs):
         halves = []
         for odd in range(2):
             s = 2 * j + odd
             at_x = jnp.clip(offset_ref[0, 0, 0, s] + MARGIN, 0, tile - 1)
-            step = jnp.bitwise_and(at_x, 7)
             first = jnp.right_shift(at_x, 3)
             at_y = offset_ref[1, 0, 0, s]
             turn = jnp.bitwise_and(at_y, 127)
@@ -489,13 +502,13 @@
                 ]
             )
             value = pltpu.roll(value, jnp.bitwise_and(STAMP * odd + 256 - turn, 127), 2)
-            value = pltpu.roll(value, jnp.bitwise_and(8 - step, 7), 1)
-            value = jnp.where(sub < 8 - step, value[:-1], value[1:])
-            halves.append(value.reshape(STAMP, 128))
+            halves.append(value)
         cutout = jnp.where(first_half, halves[0], halves[1])
         own = slice(128 * j, 128 * (j + 1))
         for k in range(3):
-            partial[48 + 8 * k : 56 + 8 * k, own] = fold(blurred[k, :, own] * cutout)
+            partial[48 + 8 * k : 56 + 8 * k, own] = jnp.sum(
+                shifted[k, 9 * j : 9 * (j + 1)] * cutout, axis=0
+            )
     right = gather_sums(partial[48:72, :])
     right = right[0] + pltpu.roll(right[1], slots, 1) + pltpu.roll(right[2], 2 * slots, 1)
     rights[me] = weight * right
@@ -601,6 +614,7 @@
             pltpu.VMEM((3, STAMP, width), F32),
             pltpu.VMEM((width, 2 * tile), BF16),
             pltpu.VMEM((rows // 8, 2, 8, 128), F32),
+            pltpu.VMEM((3, 9 * (slots // 2), 8, 128), F32),
             pltpu.VMEM((72, width), F32),
             pltpu.VMEM((peers + 1, 8, 128), F32),
             pltpu.VMEM((peers + 1, 1, 128), F32),

time: 16.3 us -> 16.3 us (level)
  no operation moved by 1% of the time
where the time goes in v6:
time: 16.3 us; the launch traced here: 16.1 us
  Pallas kernels  14.2 us (87%)
  between operations  1.93 us (12%)
    pallas_call x1, Pallas kernels, shards(): pl.pallas_call(kernel, out_shape=(pltpu.VMEM((16, 128), F32), pltpu.VMEM(...  13.5 us
    pallas_call x1, Pallas kernels, shards(): pl.pallas_call(finish, out_shape=(jax.ShapeDtypeStruct((3, 1, 1, slots),...  0.72 us

profile of v6, /device:TPU:24, one launch (start us, length us, event | category | flops | bytes accessed | tf_op | source)
XLA Modules:
  0.0 16.1 jit_solution(16045464150909969473)
XLA Ops:
  1.9 13.5 %photometry.1 = (f32[16,128]{1,0:T(8,128)S(1)}, f32[1,256,256]{2,1,0:T(8,128)S(1)}) custom-call(f32[1,256,256]{2,1,0:T(8,128)} %image_hbm.1, f32[1,2,15]{2,1,0:T(2,128)} %taps_hbm.1, f32[1]{0:T(128)S(6)} %copy.11.weight_ref, f32[1,1,16]{2,1,0:T(1,128)} %flux_hbm.1, f32[2,1,1,16]{3,2,1,0:T(1,128)} %shift_hbm.1, f32[1,1,16]{2,1,0:T(1,128)} %radius_hbm.1, ...), custom_call_target="tpu_custom_call" | custom-call | tf_op jit(solution)/shard_map/photometry/pallas_call | solution.py:596
  15.4 0.7 %finish.1 = (f32[3,1,1,16]{3,2,1,0:T(1,128)}, f32[1,256,256]{2,1,0:T(8,128)}) custom-call(f32[16,128]{1,0:T(8,128)S(1)} %get-tuple-element.4.sums_ref, f32[1,256,256]{2,1,0:T(8,128)S(1)} %get-tuple-element.5.remain_ref), custom_call_target="tpu_custom_call" | custom-call | tf_op jit(solution)/shard_map/finish/pallas_call | solution.py:644
